TPU v7x, 256 devices: a whole 4x4x8 slice. The times are simulated.
256 devices in a mesh: node: 128 (over x, z, y), rel: 2 (over core).
Axes of the slice: x: 4, y: 4, z: 8, core: 2. Of those that a mesh axis runs over, the one named last changes fastest.
Arguments:
- node_state: bfloat16 [65536, 128], P('node'), may hold values from -6 to 6
- send_list: int32 [128, 128], P('node'), may hold values from 0 to 3
- tile_weight: bfloat16 [128, 2, 192, 128, 128], P('node', 'rel'), may hold values from -0.078125 to 0.078125
- tile_slot: int32 [128, 2, 192], P('node', 'rel'), may hold values from 0 to 127
- tile_dst: int32 [128, 2, 192], P('node', 'rel'), may hold values from 0 to 3
- tile_rel: int32 [128, 2, 192], P('node', 'rel'), may hold values from 0 to 534
- live_groups: int32 [128, 2], P('node', 'rel'), may hold values from 1 to 12, as said below
- query_rel: int32 [4], replicated, may hold values from 0 to 534
- query_head: int32 [4], replicated, may hold values from 0 to 65535
- rel_table: float32 [535, 32], replicated, may hold values from -6 to 6
- rel_proj: bfloat16 [2, 32, 17120], replicated, may hold values from -1 to 1
- upd_weight: float32 [2, 32, 32], replicated, may hold values from -1 to 1
- cotangent: bfloat16 [65536, 128], P('node'), may hold values from -6 to 6
Outputs:
- final_state: bfloat16 [65536, 128], P('node')
- grad_state: float32 [65536, 128], P('node')
- grad_proj: bfloat16 [2, 32, 17120], replicated
- grad_upd: float32 [2, 32, 32], replicated
Inputs may be any that keep to these rules, and one draw needn't show every extreme that they name: `live_groups`: of the two devices of one chip, one has more than 6 live groups and the other 6 or fewer; some device has all 12.
All inputs are finite; a program needn't handle non-finite values.
Results may differ from a plain program's by a relative error of at most 0.009.
Values may be sent and summed in bfloat16 or wider, within the bound.
No kernel may reach another device: no remote copies, remote signals or barrier semaphores. Data moves between devices by JAX's collectives and lax.ppermute only.
A program may use at most 128 MiB of HBM per device.

v0:
```python
import functools

import jax
import jax.numpy as jnp
from jax import lax
from jax.experimental import pallas as pl
from jax.experimental.pallas import tpu as pltpu
from jax.sharding import Mesh
from jax.sharding import PartitionSpec as P

H = 32
R = 535
BLK = 128
HB = BLK // 2
Q = 4
L = 2
GROUP = 16
NB_DEV = 4
COLS = Q * H
ROWS = NB_DEV * HB
R8 = 536
REL_ROWS = R8 + H
F32 = jnp.float32
BF16 = jnp.bfloat16
EXACT_MATMUL = lax.Precision.HIGHEST
VMEM_LIMIT = 48 * 1024 * 1024
SWAP = [(0, 1), (1, 0)]
SMEM_SPEC = pl.BlockSpec(memory_space=pltpu.SMEM)
VMEM_SPEC = pl.BlockSpec(memory_space=pltpu.VMEM)
ANY_SPEC = pl.BlockSpec(memory_space=pl.ANY)


def grid_dims(node_count):
    if node_count == 128:
        return (4, 8, 4)
    return (2, node_count // 4, 2)


def params():
    return pltpu.CompilerParams(vmem_limit_bytes=VMEM_LIMIT)


def query_vectors(rel_table, query_rel):
    relation_ids = jnp.arange(R, dtype=jnp.int32)
    picked = (query_rel[:, None] == relation_ids[None, :]).astype(F32)
    return jnp.dot(picked, rel_table, precision=EXACT_MATMUL)


def relation_table(query_vec, proj):
    flat_rows = jnp.dot(query_vec, proj.astype(F32), precision=EXACT_MATMUL)
    table = flat_rows.reshape(Q, R, H).transpose(1, 0, 2).reshape(R, COLS)
    return jnp.pad(table, ((0, R8 - R), (0, 0)))


def split_kernel(pos, w_ref, f_keep, f_send, b_keep, b_send):
    core = pos[3]
    own = pl.multiple_of(core * HB, HB)
    other = pl.multiple_of((1 - core) * HB, HB)
    f_keep[...] = w_ref[:, pl.ds(own, HB), :]
    f_send[...] = w_ref[:, pl.ds(other, HB), :]
    for t in range(w_ref.shape[0]):
        flipped = w_ref[t].T
        low, high = flipped[:HB], flipped[HB:]
        b_keep[t] = jnp.where(core == 0, low, high)
        b_send[t] = jnp.where(core == 0, high, low)


def split_weights(pos, weights):
    tiles = weights.shape[0]
    half = jax.ShapeDtypeStruct((tiles, HB, BLK), BF16)
    spec = pl.BlockSpec((GROUP, HB, BLK), lambda g: (g, 0, 0))
    return pl.pallas_call(
        split_kernel,
        out_shape=(half,) * 4,
        grid=(tiles // GROUP,),
        in_specs=[SMEM_SPEC, pl.BlockSpec((GROUP, BLK, BLK), lambda g: (g, 0, 0))],
        out_specs=[spec] * 4,
        compiler_params=params(),
        cost_estimate=pl.CostEstimate(
            flops=0, bytes_accessed=tiles * BLK * BLK * 2 * 3, transcendentals=0
        ),
        name="split_weights",
    )(pos, weights)


def provide_kernel(dims, pos, sends, column, out):
    nx, nz, ny = dims
    z = pos[1]
    nodes = nx * nz * ny
    for owner in range(nz):
        for d in range(nx * ny):
            reader = (d // ny) * (nz * ny) + z * ny + d % ny
            block = sends[owner * nodes + reader]
            start = pl.multiple_of(block * HB, HB)
            out[d, owner] = column[owner, pl.ds(start, HB), :]


def provide(dims, pos, sends, column):
    nx, nz, ny = dims
    return pl.pallas_call(
        functools.partial(provide_kernel, dims),
        out_shape=jax.ShapeDtypeStruct((nx * ny, nz, HB, COLS), BF16),
        in_specs=[SMEM_SPEC, SMEM_SPEC, VMEM_SPEC],
        out_specs=VMEM_SPEC,
        compiler_params=params(),
        name="provide",
    )(pos, sends, column)


def start_weights(meta, tiles, weights, buffer, sems):
    groups = tiles // GROUP
    for source in range(2):
        live = meta[(source * 4 + 3) * tiles]
        for g in range(groups):

            @pl.when(g < live)
            def _(source=source, g=g):
                pltpu.make_async_copy(
                    weights[source].at[pl.ds(g * GROUP, GROUP)],
                    buffer.at[source * groups + g],
                    sems.at[source * groups + g],
                ).start()


def over_tiles(meta, tiles, weights, buffer, sems, one_tile):
    groups = tiles // GROUP
    for source in range(2):
        live = meta[(source * 4 + 3) * tiles]
        base = source * 4 * tiles

        def one_group(g, carry, source=source, base=base):
            place = source * groups + g
            pltpu.make_async_copy(
                weights[source].at[pl.ds(g * GROUP, GROUP)],
                buffer.at[place],
                sems.at[place],
            ).wait()
            for t in range(GROUP):
                at = base + g * GROUP + t
                one_tile(
                    buffer[place, t],
                    meta[at],
                    meta[at + tiles],
                    meta[at + 2 * tiles],
                )
            return carry

        lax.fori_loop(0, live, one_group, 0)


def update_terms(aggregate, grad_pre, block_mask):
    product = jnp.dot(aggregate.T, grad_pre, precision=EXACT_MATMUL, preferred_element_type=F32)
    product = product * block_mask
    total = product[:H]
    for q in range(1, Q):
        total = total + product[q * H : (q + 1) * H]
    return total


def before_backward(grad, pre, aggregate, upd_t, block_mask, gagg_ref, upd_ref):
    sigma = jax.nn.sigmoid(pre)
    grad_pre = grad * (sigma * (1.0 + pre * (1.0 - sigma)))
    gagg_ref[...] = jnp.dot(
        grad_pre, upd_t, precision=EXACT_MATMUL, preferred_element_type=F32
    ).astype(BF16)
    upd_ref[...] = update_terms(aggregate, grad_pre, block_mask)


def forward_kernel(last, tiles, meta, pos, rec_own, rec_other, w_own, w_other, table, bound,
                   upd, state, *refs):
    if last:
        cotangent, upd_t, block_mask = refs[:3]
        next_ref, gagg_ref, upd_ref, rec, buffer, acc, w_sems, r_sems = refs[3:]
    else:
        next_ref, agg_ref, pre_ref, rec, buffer, acc, w_sems, r_sems = refs
    own = pl.multiple_of(pos[3] * HB, HB)
    other = pl.multiple_of((1 - pos[3]) * HB, HB)
    copies = [
        pltpu.make_async_copy(rec_own, rec.at[:, pl.ds(own, HB), :], r_sems.at[0]),
        pltpu.make_async_copy(rec_other, rec.at[:, pl.ds(other, HB), :], r_sems.at[1]),
    ]
    for copy in copies:
        copy.start()
    start_weights(meta, tiles, (w_own, w_other), buffer, w_sems)
    acc[...] = jnp.zeros_like(acc)
    for copy in copies:
        copy.wait()

    def one_tile(weight, slot, dst, rel):
        message = jnp.dot(weight, rec[slot], preferred_element_type=F32)
        acc[dst] = acc[dst] + message * table[pl.ds(rel, 1), :]

    over_tiles(meta, tiles, (w_own, w_other), buffer, w_sems, one_tile)
    aggregate = acc[...].reshape(ROWS, COLS) + bound[...]
    pre = jnp.dot(aggregate, upd[...], precision=EXACT_MATMUL, preferred_element_type=F32)
    next_ref[...] = (state[...].astype(F32) + pre * jax.nn.sigmoid(pre)).astype(BF16)
    if last:
        before_backward(
            cotangent[...].astype(F32), pre, aggregate, upd_t[...], block_mask[...],
            gagg_ref, upd_ref,
        )
    else:
        agg_ref[...] = aggregate
        pre_ref[...] = pre


def forward(last, meta, pos, rec_own, rec_other, w_own, w_other, table, bound, upd, state, more):
    slots, tiles = rec_own.shape[0], w_own.shape[0]
    places = 2 * (tiles // GROUP)
    rows16 = jax.ShapeDtypeStruct((ROWS, COLS), BF16)
    rows32 = jax.ShapeDtypeStruct((ROWS, COLS), F32)
    if last:
        outs = (rows16, rows16, jax.ShapeDtypeStruct((H, COLS), F32))
    else:
        outs = (rows16, rows32, rows32)
    return pl.pallas_call(
        functools.partial(forward_kernel, last, tiles),
        out_shape=outs,
        in_specs=[SMEM_SPEC, SMEM_SPEC] + [ANY_SPEC] * 4 + [VMEM_SPEC] * (4 + len(more)),
        out_specs=(VMEM_SPEC,) * 3,
        scratch_shapes=[
            pltpu.VMEM((slots, BLK, COLS), BF16),
            pltpu.VMEM((places, GROUP, HB, BLK), BF16),
            pltpu.VMEM((NB_DEV, HB, COLS), F32),
            pltpu.SemaphoreType.DMA((places,)),
            pltpu.SemaphoreType.DMA((2,)),
        ],
        compiler_params=params(),
        name="forward_last" if last else "forward_first",
    )(meta, pos, rec_own, rec_other, w_own, w_other, table, bound, upd, state, *more)


def backward_kernel(dims, tiles, chunk, meta, pos, rec_own, w_own, w_other, gagg_own,
                    gagg_other, table, upd_sum, *refs):
    passed, refs = refs[:-8], refs[-8:]
    out, rec, buffer, slot_acc, rel_acc, gagg, w_sems, r_sem = refs
    nx, nz, ny = dims
    copy = pltpu.make_async_copy(rec_own, rec, r_sem.at[0])
    copy.start()
    start_weights(meta, tiles, (w_own, w_other), buffer, w_sems)
    own = pl.multiple_of(pos[3] * HB, HB)
    other = pl.multiple_of((1 - pos[3]) * HB, HB)
    gagg[:, pl.ds(own, HB), :] = gagg_own[...].reshape(NB_DEV, HB, COLS)
    gagg[:, pl.ds(other, HB), :] = gagg_other[...].reshape(NB_DEV, HB, COLS)
    rel_acc[...] = jnp.zeros_like(rel_acc)
    rel_acc[R8 : R8 + H, :] = upd_sum[...]

    def clear(d, carry):
        slot_acc[pl.ds(d * nz, nz)] = jnp.zeros((nz, HB, COLS), F32)
        return carry

    lax.fori_loop(0, nx * ny, clear, 0)
    copy.wait()

    def one_tile(weight, slot, dst, rel):
        back = jnp.dot(weight, gagg[dst], preferred_element_type=F32)
        row = pl.ds(rel, 1)
        slot_acc[slot] = slot_acc[slot] + back * table[row, :]
        terms = jnp.sum(back * rec[slot].astype(F32), axis=0, keepdims=True)
        rel_acc[row, :] = rel_acc[row, :] + terms

    over_tiles(meta, tiles, (w_own, w_other), buffer, w_sems, one_tile)

    def put(d, carry):
        out[d, : nz * HB, :] = slot_acc[pl.ds(d * nz, nz)].reshape(nz * HB, COLS).astype(BF16)
        start = pl.multiple_of(d * chunk, 16)
        out[d, nz * HB : nz * HB + chunk, :] = rel_acc[pl.ds(start, chunk), :].astype(BF16)
        for part in passed:
            out[d, nz * HB + chunk :, :] = part[...].astype(BF16)
        return carry

    lax.fori_loop(0, nx * ny, put, 0)


def backward(dims, chunk, meta, pos, rec_own, w_own, w_other, gagg_own, gagg_other, table, upd_sum,
             passed):
    nx, nz, ny = dims
    slots, tiles = rec_own.shape[0], w_own.shape[0]
    places = 2 * (tiles // GROUP)
    return pl.pallas_call(
        functools.partial(backward_kernel, dims, tiles, chunk),
        out_shape=jax.ShapeDtypeStruct(
            (nx * ny, nz * HB + chunk * (1 + len(passed)), COLS), BF16
        ),
        in_specs=[SMEM_SPEC, SMEM_SPEC] + [ANY_SPEC] * 3 + [VMEM_SPEC] * (4 + len(passed)),
        out_specs=VMEM_SPEC,
        scratch_shapes=[
            pltpu.VMEM((slots, HB, COLS), BF16),
            pltpu.VMEM((places, GROUP, HB, BLK), BF16),
            pltpu.VMEM((slots, HB, COLS), F32),
            pltpu.VMEM((nx * ny * chunk, COLS), F32),
            pltpu.VMEM((NB_DEV, BLK, COLS), BF16),
            pltpu.SemaphoreType.DMA((places,)),
            pltpu.SemaphoreType.DMA((1,)),
        ],
        compiler_params=params(),
        name="backward",
    )(meta, pos, rec_own, w_own, w_other, gagg_own, gagg_other, table, upd_sum, *passed)


def combine_kernel(dims, chunk, pos, sends, arrived, out, *refs):
    acc = refs[-1]
    nx, nz, ny = dims
    z = pos[1]
    nodes = nx * nz * ny
    acc[...] = jnp.zeros_like(acc)
    rel = jnp.zeros((chunk, COLS), F32)
    for s in range(nx * ny):
        sender = (s // ny) * (nz * ny) + z * ny + s % ny
        for owner in range(nz):
            block = sends[owner * nodes + sender]
            acc[owner, block] = acc[owner, block] + arrived[
                s, owner * HB : (owner + 1) * HB, :
            ].astype(F32)
        rel = rel + arrived[s, nz * HB : nz * HB + chunk, :].astype(F32)
        for whole in refs[:-1]:
            whole[s * chunk : (s + 1) * chunk, :] = arrived[s, nz * HB + chunk :, :].astype(F32)
    for owner in range(nz):
        out[owner, :ROWS, :] = acc[owner].reshape(ROWS, COLS).astype(BF16)
        out[owner, ROWS:, :] = rel.astype(BF16)


def combine(dims, chunk, pos, sends, arrived):
    nx, nz, ny = dims
    outs = [jax.ShapeDtypeStruct((nz, ROWS + chunk, COLS), BF16)]
    if arrived.shape[1] > nz * HB + chunk:
        outs.append(jax.ShapeDtypeStruct((nx * ny * chunk, COLS), F32))
    return pl.pallas_call(
        functools.partial(combine_kernel, dims, chunk),
        out_shape=outs,
        in_specs=[SMEM_SPEC, SMEM_SPEC, VMEM_SPEC],
        out_specs=[VMEM_SPEC] * len(outs),
        scratch_shapes=[pltpu.VMEM((nz, NB_DEV, HB, COLS), F32)],
        compiler_params=params(),
        name="combine",
    )(pos, sends, arrived)


def collect_kernel(more, parts, *refs):
    total = parts[0].astype(F32)
    for k in range(1, parts.shape[0]):
        total = total + parts[k].astype(F32)
    grad = refs[0][...].astype(F32) + total[:ROWS]
    if more:
        pre, aggregate, upd_t, block_mask, grad_ref, rel_ref, gagg_ref, upd_ref = refs[1:]
        before_backward(
            grad, pre[...], aggregate[...], upd_t[...], block_mask[...], gagg_ref, upd_ref
        )
    else:
        grad_ref, rel_ref = refs[1:]
    grad_ref[...] = grad
    rel_ref[...] = total[ROWS:]


def collect(chunk, parts, grad, more):
    outs = [jax.ShapeDtypeStruct((ROWS, COLS), F32), jax.ShapeDtypeStruct((chunk, COLS), F32)]
    if more:
        outs.append(jax.ShapeDtypeStruct((ROWS, COLS), BF16))
        outs.append(jax.ShapeDtypeStruct((H, COLS), F32))
    return pl.pallas_call(
        functools.partial(collect_kernel, bool(more)),
        out_shape=tuple(outs),
        in_specs=[VMEM_SPEC] * (2 + len(more)),
        out_specs=(VMEM_SPEC,) * len(outs),
        compiler_params=params(),
        name="collect_more" if more else "collect_last",
    )(parts, grad, *more)


def gather_relations(dims, rel):
    count = dims[0] * dims[2]
    copies = jnp.broadcast_to(rel[None], (count,) + rel.shape)
    parts = lax.all_to_all(copies, ("x", "y"), 0, 0, tiled=True)
    return parts.reshape(count * rel.shape[0], COLS)


def whole_rows(core, own, other):
    own, other = (v.reshape(NB_DEV, 1, HB, COLS) for v in (own, other))
    low = jnp.where(core == 0, own, other)
    high = jnp.where(core == 0, other, own)
    return jnp.concatenate([low, high], axis=1).reshape(NB_DEV * BLK, COLS)


def body(dims, node_state, send_list, tile_weight, tile_slot, tile_dst, tile_rel, live_groups,
         query_rel, query_head, rel_table, rel_proj, upd_weight, cotangent):
    nx, nz, ny = dims
    nodes = nx * nz * ny
    chunk = -(-REL_ROWS // (nx * ny * 16)) * 16
    x, z, y, core = (lax.axis_index(a) for a in ("x", "z", "y", "c"))
    node = (x * nz + z) * ny + y
    pos = jnp.stack([x, z, y, core]).astype(jnp.int32)
    tiles = tile_weight.shape[2]

    def own_half(rows):
        return lax.dynamic_index_in_dim(
            rows.reshape(NB_DEV, 2, HB, COLS), core, 1, keepdims=False
        ).reshape(ROWS, COLS)

    def swap(value):
        return lax.ppermute(value, "c", SWAP)

    def column_of(rows):
        copies = jnp.broadcast_to(rows[None], (nz,) + rows.shape)
        return lax.all_to_all(copies, "z", 0, 0, tiled=True)

    state = own_half(node_state)
    listed = jnp.pad(send_list.astype(BF16), ((0, 15), (0, COLS - nodes)))
    column = column_of(jnp.concatenate([state, listed]))

    slot = tile_slot[0, 0]
    slot = ((slot // (nz * ny)) * ny + slot % ny) * nz + (slot // ny) % nz
    live = jnp.broadcast_to(live_groups[0, 0], (tiles,))
    meta = jnp.stack([slot, tile_dst[0, 0], tile_rel[0, 0], live])
    meta = jnp.stack([meta, swap(meta)]).reshape(-1)

    lane_block = jnp.arange(COLS, dtype=jnp.int32) // H
    block_mask = (lane_block[:, None] == lane_block[None, :]).astype(F32)
    upd = [jnp.tile(upd_weight[l], (Q, Q)) * block_mask for l in range(L)]
    upd_t = [u.T for u in upd]
    cot = own_half(cotangent)
    column, meta, upd, upd_t, block_mask, cot = lax.optimization_barrier(
        (column, meta, upd, upd_t, block_mask, cot)
    )
    sends = column[:, ROWS, :nodes].astype(jnp.int32).reshape(-1)
    outgoing = provide(dims, pos, sends, column)
    outgoing, later, query_rel = lax.optimization_barrier((outgoing, pos, query_rel))
    f_own, f_send, b_own, b_send = split_weights(later, tile_weight[0, 0])
    f_other, b_other = swap(f_send), swap(b_send)
    query_vec = query_vectors(rel_table, query_rel)
    row_ids = node * (NB_DEV * BLK) + (
        jnp.arange(NB_DEV, dtype=jnp.int32)[:, None] * BLK
        + core * HB
        + jnp.arange(HB, dtype=jnp.int32)[None, :]
    ).reshape(ROWS)
    matches = (row_ids[:, None] == query_head[None, :]).astype(F32)
    bound = (matches[:, :, None] * query_vec[None, :, :]).reshape(ROWS, COLS)

    received, tables = [], []
    for l in range(L):
        if l:
            outgoing = provide(dims, pos, sends, column_of(state))
            outgoing, vectors = lax.optimization_barrier((outgoing, query_vec))
        else:
            vectors = query_vec
        rec_own = lax.all_to_all(outgoing, ("x", "y"), 0, 0, tiled=True)
        table = relation_table(vectors, rel_proj[l])
        if l:
            rec_own, table = lax.optimization_barrier((rec_own, table))
        else:
            rec_own, table, bound, f_own, f_other, b_own, b_other = lax.optimization_barrier(
                (rec_own, table, bound, f_own, f_other, b_own, b_other)
            )
        tables.append(table)
        rec_own = rec_own.reshape(nodes, HB, COLS)
        received.append(rec_own)
        last = l == L - 1
        more = (cot, upd_t[l], block_mask) if last else ()
        made = forward(
            last, meta, pos, rec_own, swap(rec_own), f_own, f_other, tables[l], bound, upd[l],
            state, more,
        )
        state = made[0]
        if last:
            gagg, upd_sum = made[1:]
        else:
            agg0, pre0 = made[1:]

    grad = cot
    passed = ()
    relations = [None] * L
    for l in reversed(range(L)):
        sent = backward(
            dims, chunk, meta, pos, received[l], b_own, b_other, gagg, swap(gagg), tables[l],
            upd_sum, passed,
        )
        arrived = lax.all_to_all(sent, ("x", "y"), 0, 0, tiled=True)
        combined, *whole = combine(dims, chunk, pos, sends, arrived)
        parts = lax.all_to_all(combined, "z", 0, 0, tiled=True)
        more = (pre0, agg0, upd_t[0], block_mask) if l else ()
        made = collect(chunk, parts, grad, more)
        grad, rel = made[:2]
        if l:
            gagg, upd_sum = made[2:]
        rel = rel + swap(rel)
        passed = (rel,) if l else ()
        if whole:
            relations[l + 1] = whole[0]
    relations[0] = gather_relations(dims, rel)

    scale_factor = float(nodes * NB_DEV * BLK) ** (-0.5)
    projs = []
    upds = []
    for l in range(L):
        projs.append(
            jnp.einsum(
                "qh,rqk->hrk",
                query_vec,
                relations[l][:R].reshape(R, Q, H),
                precision=EXACT_MATMUL,
            ).reshape(H, R * H)
            * scale_factor
        )
        upds.append(relations[l][R8 : R8 + H].reshape(H, Q, H).sum(1))
    final_state = whole_rows(core, state, swap(state))
    grad_state = whole_rows(core, grad, swap(grad))
    return (
        final_state,
        grad_state,
        jnp.stack(projs).astype(BF16),
        jnp.stack(upds) * scale_factor,
    )


def solution(mesh):
    dims = grid_dims(mesh.shape["node"])
    fine = Mesh(mesh.devices.reshape(*dims, 2), ("x", "z", "y", "c"))
    node = ("x", "z", "y")
    return jax.shard_map(
        functools.partial(body, dims),
        mesh=fine,
        in_specs=(
            P(node, None),
            P(node, None),
            P(node, "c", None, None, None),
            P(node, "c", None),
            P(node, "c", None),
            P(node, "c", None),
            P(node, "c"),
            P(),
            P(),
            P(),
            P(),
            P(),
            P(node, None),
        ),
        out_specs=(P(node, None), P(node, None), P(), P()),
        check_vma=False,
    )
```

profile of v0, /device:TPU:1, one launch (start us, length us, event | category | flops | bytes accessed | tf_op | source)
XLA Modules:
  0.0 321.8 jit_solution(2395893972194587038)
XLA Ops:
  7.8 6.5 %all-to-all-start = ((bf16[8,272,128]{2,1,0:T(8,128)(2,1)}), bf16[8,272,128]{2,1,0:T(8,128)(2,1)S(1)}, u32[]{:S(2)}, u32[]{:S(2)}) async-start(bf16[8,272,128]{2,1,0:T(8,128)(2,1)} %broadcast_in_dim.6), calls=%async_computation | async-start | bytes 1114112 | tf_op jit(solution)/shard_map/all_to_all | solution.py:404
  15.8 17.1 %all-to-all-done.column = bf16[8,272,128]{2,1,0:T(8,128)(2,1)S(1)} async-done(((bf16[8,272,128]{2,1,0:T(8,128)(2,1)}), bf16[8,272,128]{2,1,0:T(8,128)(2,1)S(1)}, u32[]{:S(2)}, u32[]{:S(2)}) %all-to-all-start) | async-done | bytes 557088 | tf_op jit(solution)/shard_map/all_to_all | solution.py:404
  35.1 6.8 %all-to-all-start.1 = ((bf16[16,8,64,128]{3,2,1,0:T(8,128)(2,1)}), bf16[16,8,64,128]{3,2,1,0:T(8,128)(2,1)S(1)}, u32[]{:S(2)}, u32[]{:S(2)}) async-start(bf16[16,8,64,128]{3,2,1,0:T(8,128)(2,1)} %copy-done.3), calls=%async_computation.1 | async-start | bytes 4194304 | tf_op jit(solution)/shard_map/all_to_all | solution.py:445
  41.9 10.7 %split_weights.1 = (bf16[192,64,128]{2,1,0:T(8,128)(2,1)S(1)}, bf16[192,64,128]{2,1,0:T(8,128)(2,1)}, bf16[192,64,128]{2,1,0:T(8,128)(2,1)}, bf16[192,64,128]{2,1,0:T(8,128)(2,1)}) custom-call(s32[4]{0:T(128)S(1)} %pad_add_fusion.1.pos, bf16[192,128,128]{2,1,0:T(8,128)(2,1)} %bitcast.116), custom_call_target="tpu_custom_call" | custom-call | bytes 18874368 | tf_op jit(solution)/shard_map/split_weights/pallas_call | solution.py:72
  56.9 5.6 %dot_general.33 = bf16[535,32,32]{1,0,2:T(8,128)(2,1)} reshape(bf16[17120,32]{0,1:T(8,128)(2,1)} %get-tuple-element.85) | data formatting | bytes 2191360 | tf_op jit(solution)/shard_map/dot_general | solution.py:50
  62.5 5.0 %copy.44 = bf16[535,32,32]{0,2,1:T(8,128)(2,1)} copy(bf16[535,32,32]{1,0,2:T(8,128)(2,1)} %dot_general.33) | data formatting | bytes 2191360 | tf_op jit(solution)/shard_map/dot_general | solution.py:50
  73.4 3.8 %collective-permute-done.3.rec_other = bf16[128,64,128]{2,1,0:T(8,128)(2,1)S(1)} collective-permute-done((bf16[128,64,128]{2,1,0:T(8,128)(2,1)S(1)}, bf16[128,64,128]{2,1,0:T(8,128)(2,1)S(1)}, u32[]{:S(2)}, u32[]{:S(2)}) %collective-permute-start.3) | collective-permute-done | bytes 2097184 | tf_op jit(solution)/shard_map/ppermute | solution.py:400
  77.2 6.0 %forward_first.1 = (bf16[256,128]{1,0:T(8,128)(2,1)S(1)}, f32[256,128]{1,0:T(8,128)S(1)}, f32[256,128]{1,0:T(8,128)S(1)}) custom-call(s32[1536]{0:T(1024)S(1)} %reshape.421.meta, s32[4]{0:T(128)S(1)} %pad_add_fusion.1.pos, bf16[128,64,128]{2,1,0:T(8,128)(2,1)S(1)} %bitcast.104, bf16[128,64,128]{2,1,0:T(8,128)(2,1)S(1)} %collective-permute-done.3.rec_other, ...), custom_call_target="tpu_custom_call" | custom-call | tf_op jit(solution)/shard_map/forward_first/pallas_call | solution.py:216
  84.5 20.4 %all_to_all.45.column = bf16[8,256,128]{2,1,0:T(8,128)(2,1)S(1)} all-to-all(bf16[8,256,128]{2,1,0:T(8,128)(2,1)S(1)} %broadcast_in_dim.7), channel_id=1, replica_groups=mesh['x'=4,'z'=8,'y'=4,'c'=2] {'z'}, dimensions={0} | all-to-all | bytes 1048576 | tf_op jit(solution)/shard_map/all_to_all | solution.py:404
  107.0 5.8 %all-to-all-start.3 = ((bf16[16,8,64,128]{3,2,1,0:T(8,128)(2,1)}), bf16[16,8,64,128]{3,2,1,0:T(8,128)(2,1)}, u32[]{:S(2)}, u32[]{:S(2)}) async-start(bf16[16,8,64,128]{3,2,1,0:T(8,128)(2,1)} %copy-done.4), calls=%async_computation.3 | async-start | bytes 4194304 | tf_op jit(solution)/shard_map/all_to_all | solution.py:445
  112.8 5.6 %dot_general.36 = bf16[535,32,32]{1,0,2:T(8,128)(2,1)} reshape(bf16[17120,32]{0,1:T(8,128)(2,1)} %get-tuple-element.84) | data formatting | bytes 2191360 | tf_op jit(solution)/shard_map/dot_general | solution.py:50
  118.4 5.0 %copy.48 = bf16[535,32,32]{0,2,1:T(8,128)(2,1)} copy(bf16[535,32,32]{1,0,2:T(8,128)(2,1)} %dot_general.36) | data formatting | bytes 2191360 | tf_op jit(solution)/shard_map/dot_general | solution.py:50
  127.3 14.6 %all-to-all-done.3 = bf16[16,8,64,128]{3,2,1,0:T(8,128)(2,1)} async-done(((bf16[16,8,64,128]{3,2,1,0:T(8,128)(2,1)}), bf16[16,8,64,128]{3,2,1,0:T(8,128)(2,1)}, u32[]{:S(2)}, u32[]{:S(2)}) %all-to-all-start.3) | async-done | bytes 2097184 | tf_op jit(solution)/shard_map/all_to_all | solution.py:445
  144.5 4.0 %collective-permute-done.4.rec_other = bf16[128,64,128]{2,1,0:T(8,128)(2,1)} collective-permute-done((bf16[128,64,128]{2,1,0:T(8,128)(2,1)}, bf16[128,64,128]{2,1,0:T(8,128)(2,1)}, u32[]{:S(2)}, u32[]{:S(2)}) %collective-permute-start.4) | collective-permute-done | bytes 2097184 | tf_op jit(solution)/shard_map/ppermute | solution.py:400
  148.5 7.9 %forward_last.1 = (bf16[256,128]{1,0:T(8,128)(2,1)S(1)}, bf16[256,128]{1,0:T(8,128)(2,1)S(1)}, f32[32,128]{1,0:T(8,128)S(1)}) custom-call(s32[1536]{0:T(1024)S(1)} %reshape.421.meta, s32[4]{0:T(128)S(1)} %pad_add_fusion.1.pos, bf16[128,64,128]{2,1,0:T(8,128)(2,1)} %bitcast.32.rec_own, bf16[128,64,128]{2,1,0:T(8,128)(2,1)} %collective-permute-done.4.rec_other, ...), custom_call_target="tpu_custom_call" | custom-call | tf_op jit(solution)/shard_map/forward_last/pallas_call | solution.py:216
  157.9 6.9 %backward.2 = bf16[16,560,128]{2,1,0:T(8,128)(2,1)S(1)} custom-call(s32[1536]{0:T(1024)S(1)} %reshape.421.meta, s32[4]{0:T(128)S(1)} %pad_add_fusion.1.pos, bf16[128,64,128]{2,1,0:T(8,128)(2,1)} %bitcast.32.rec_own, bf16[192,64,128]{2,1,0:T(8,128)(2,1)} %get-tuple-element.69.w_own, bf16[192,64,128]{2,1,0:T(8,128)(2,1)} %collective-permute-done.2.w_other, ...), custom_call_target="tpu_custom_call" | custom-call | tf_op jit(solution)/shard_map/backward/pallas_call | solution.py:280
  164.8 37.5 %all_to_all.46.arrived = bf16[16,560,128]{2,1,0:T(8,128)(2,1)S(1)} all-to-all(bf16[16,560,128]{2,1,0:T(8,128)(2,1)S(1)} %backward.2), channel_id=1, replica_groups=mesh['x'=4,'z'=8,'y'=4,'c'=2] {'x','y'}, dimensions={0} | all-to-all | bytes 4587520 | tf_op jit(solution)/shard_map/all_to_all | solution.py:476
  204.7 3.5 %all-to-all-start.5 = ((bf16[8,304,128]{2,1,0:T(8,128)(2,1)}), bf16[8,304,128]{2,1,0:T(8,128)(2,1)S(1)}, u32[]{:S(2)}, u32[]{:S(2)}) async-start(bf16[8,304,128]{2,1,0:T(8,128)(2,1)} %combine.2), calls=%async_computation.5 | async-start | bytes 1245184 | tf_op jit(solution)/shard_map/all_to_all | solution.py:478
  208.4 18.3 %all-to-all-done.5.parts = bf16[8,304,128]{2,1,0:T(8,128)(2,1)S(1)} async-done(((bf16[8,304,128]{2,1,0:T(8,128)(2,1)}), bf16[8,304,128]{2,1,0:T(8,128)(2,1)S(1)}, u32[]{:S(2)}, u32[]{:S(2)}) %all-to-all-start.5) | async-done | bytes 622624 | tf_op jit(solution)/shard_map/all_to_all | solution.py:478
  232.9 5.5 %backward.3 = bf16[16,608,128]{2,1,0:T(8,128)(2,1)S(1)} custom-call(s32[1536]{0:T(1024)S(1)} %reshape.421.meta, s32[4]{0:T(128)S(1)} %pad_add_fusion.1.pos, bf16[128,64,128]{2,1,0:T(8,128)(2,1)S(1)} %bitcast.105, bf16[192,64,128]{2,1,0:T(8,128)(2,1)} %get-tuple-element.69.w_own, bf16[192,64,128]{2,1,0:T(8,128)(2,1)} %collective-permute-done.2.w_other, ...), custom_call_target="tpu_custom_call" | custom-call | tf_op jit(solution)/shard_map/backward/pallas_call | solution.py:280
  238.4 36.5 %all_to_all.47.arrived = bf16[16,608,128]{2,1,0:T(8,128)(2,1)S(1)} all-to-all(bf16[16,608,128]{2,1,0:T(8,128)(2,1)S(1)} %backward.3), channel_id=1, replica_groups=mesh['x'=4,'z'=8,'y'=4,'c'=2] {'x','y'}, dimensions={0} | all-to-all | bytes 4980736 | tf_op jit(solution)/shard_map/all_to_all | solution.py:476
  283.3 15.6 %all-to-all-done.7.parts = bf16[8,304,128]{2,1,0:T(8,128)(2,1)S(1)} async-done(((bf16[8,304,128]{2,1,0:T(8,128)(2,1)}), bf16[8,304,128]{2,1,0:T(8,128)(2,1)S(1)}, u32[]{:S(2)}, u32[]{:S(2)}) %all-to-all-start.7) | async-done | bytes 622624 | tf_op jit(solution)/shard_map/all_to_all | solution.py:478
  303.7 3.9 %all-to-all-start.8 = ((f32[16,48,128]{2,1,0:T(8,128)}), f32[16,48,128]{2,1,0:T(8,128)S(1)}, u32[]{:S(2)}, u32[]{:S(2)}) async-start(f32[16,48,128]{2,1,0:T(8,128)} %broadcast_in_dim.8), calls=%async_computation.8 | async-start | bytes 786432 | tf_op jit(solution)/shard_map/all_to_all | solution.py:373
  310.5 6.1 %all-to-all-done.8 = f32[16,48,128]{2,1,0:T(8,128)S(1)} async-done(((f32[16,48,128]{2,1,0:T(8,128)}), f32[16,48,128]{2,1,0:T(8,128)S(1)}, u32[]{:S(2)}, u32[]{:S(2)}) %all-to-all-start.8) | async-done | bytes 393248 | tf_op jit(solution)/shard_map/all_to_all | solution.py:373
  (133 shorter events, 61.6 us)
Async XLA Ops:
  0.6 6.2 %copy-start = (bf16[512,128]{1,0:T(8,128)(2,1)S(1)}, bf16[512,128]{1,0:T(8,128)(2,1)}, u32[]{:S(2)}) copy-start(bf16[512,128]{1,0:T(8,128)(2,1)} %param.13) | copy-start | bytes 393220
  0.6 14.7 %copy-start.14 = (s32[1,1,192]{2,1,0:T(1,128)S(1)}, s32[1,1,192]{2,1,0:T(1,128)}, u32[]{:S(2)}) copy-start(s32[1,1,192]{2,1,0:T(1,128)} %param.18) | copy-start | bytes 2308
  0.7 14.7 %copy-start.15 = (s32[1,1,192]{2,1,0:T(1,128)S(1)}, s32[1,1,192]{2,1,0:T(1,128)}, u32[]{:S(2)}) copy-start(s32[1,1,192]{2,1,0:T(1,128)} %param.17) | copy-start | bytes 2308
  0.7 14.3 %copy-start.13 = (bf16[512,128]{1,0:T(8,128)(2,1)S(1)}, bf16[512,128]{1,0:T(8,128)(2,1)}, u32[]{:S(2)}) copy-start(bf16[512,128]{1,0:T(8,128)(2,1)} %param.25) | copy-start | bytes 393220
  2.9 12.8 %collective-permute-start = (s32[4,192]{1,0:T(4,128)S(1)}, s32[4,192]{1,0:T(4,128)S(1)}, u32[]{:S(2)}, u32[]{:S(2)}) collective-permute-start(s32[4,192]{1,0:T(4,128)S(1)} %add_add_fusion), channel_id=1, source_target_pairs={{0,1},{1,0},{2,3},{3,2},{4,5},{5,4},{6,7},{7,6},{8,9},{9,8},{10,11... | collective-permute-start | bytes 9224 | tf_op jit(solution)/shard_map/ppermute | solution.py:400
  7.8 25.2 %all-to-all-start = ((bf16[8,272,128]{2,1,0:T(8,128)(2,1)}), bf16[8,272,128]{2,1,0:T(8,128)(2,1)S(1)}, u32[]{:S(2)}, u32[]{:S(2)}) async-start(bf16[8,272,128]{2,1,0:T(8,128)(2,1)} %broadcast_in_dim.6), calls=%async_computation | async-start | bytes 1114112 | tf_op jit(solution)/shard_map/all_to_all | solution.py:404
  35.1 35.8 %all-to-all-start.1 = ((bf16[16,8,64,128]{3,2,1,0:T(8,128)(2,1)}), bf16[16,8,64,128]{3,2,1,0:T(8,128)(2,1)S(1)}, u32[]{:S(2)}, u32[]{:S(2)}) async-start(bf16[16,8,64,128]{3,2,1,0:T(8,128)(2,1)} %copy-done.3), calls=%async_computation.1 | async-start | bytes 4194304 | tf_op jit(solution)/shard_map/all_to_all | solution.py:445
  41.8 13.2 %copy-start.11 = (bf16[2,32,17120]{2,1,0:T(8,128)(2,1)S(1)}, bf16[2,32,17120]{2,1,0:T(8,128)(2,1)}, u32[]{:S(2)}) copy-start(bf16[2,32,17120]{2,1,0:T(8,128)(2,1)} %param.23) | copy-start | bytes 6574084
  54.3 16.6 %collective-permute-start.1 = (bf16[192,64,128]{2,1,0:T(8,128)(2,1)}, bf16[192,64,128]{2,1,0:T(8,128)(2,1)}, u32[]{:S(2)}, u32[]{:S(2)}) collective-permute-start(bf16[192,64,128]{2,1,0:T(8,128)(2,1)} %get-tuple-element.50), channel_id=1, source_target_pairs={{0,1},{1,0},{2,3},{3,2},{4,5},{5,4},{6,7},{7,6},{8,9},{9,8},{10,11... | collective-permute-start | bytes 9437192 | tf_op jit(solution)/shard_map/ppermute | solution.py:400
  55.1 15.8 %collective-permute-start.2 = (bf16[192,64,128]{2,1,0:T(8,128)(2,1)}, bf16[192,64,128]{2,1,0:T(8,128)(2,1)}, u32[]{:S(2)}, u32[]{:S(2)}) collective-permute-start(bf16[192,64,128]{2,1,0:T(8,128)(2,1)} %get-tuple-element.52), channel_id=1, source_target_pairs={{0,1},{1,0},{2,3},{3,2},{4,5},{5,4},{6,7},{7,6},{8,9},{9,8},{10,11... | collective-permute-start | bytes 9437192 | tf_op jit(solution)/shard_map/ppermute | solution.py:400
  62.5 5.0 %copy-start.16 = (s32[4]{0:T(128)S(1)}, s32[4]{0:T(128)}, u32[]{:S(2)}) copy-start(s32[4]{0:T(128)} %param.20) | copy-start | bytes 52
  70.9 6.3 %collective-permute-start.3 = (bf16[128,64,128]{2,1,0:T(8,128)(2,1)S(1)}, bf16[128,64,128]{2,1,0:T(8,128)(2,1)S(1)}, u32[]{:S(2)}, u32[]{:S(2)}) collective-permute-start(bf16[128,64,128]{2,1,0:T(8,128)(2,1)S(1)} %bitcast.103), channel_id=1, source_target_pairs={{0,1},{1,0},{2,3},{3,2},{4,5},{5,4},{6,7},{7,6},{8,9},{9,8},{10,11... | collective-permute-start | bytes 6291464 | tf_op jit(solution)/shard_map/ppermute | solution.py:400
  107.0 34.9 %all-to-all-start.3 = ((bf16[16,8,64,128]{3,2,1,0:T(8,128)(2,1)}), bf16[16,8,64,128]{3,2,1,0:T(8,128)(2,1)}, u32[]{:S(2)}, u32[]{:S(2)}) async-start(bf16[16,8,64,128]{3,2,1,0:T(8,128)(2,1)} %copy-done.4), calls=%async_computation.3 | async-start | bytes 4194304 | tf_op jit(solution)/shard_map/all_to_all | solution.py:445
  141.9 6.6 %collective-permute-start.4 = (bf16[128,64,128]{2,1,0:T(8,128)(2,1)}, bf16[128,64,128]{2,1,0:T(8,128)(2,1)}, u32[]{:S(2)}, u32[]{:S(2)}) collective-permute-start(bf16[128,64,128]{2,1,0:T(8,128)(2,1)} %bitcast.32.rec_own), channel_id=1, source_target_pairs={{0,1},{1,0},{2,3},{3,2},{4,5},{5,4},{6,7},{7,6},{8,9},{9,8},{10,11... | collective-permute-start | bytes 6291464 | tf_op jit(solution)/shard_map/ppermute | solution.py:400
  156.4 1.5 collective-permute-start.6
  204.7 21.9 %all-to-all-start.5 = ((bf16[8,304,128]{2,1,0:T(8,128)(2,1)}), bf16[8,304,128]{2,1,0:T(8,128)(2,1)S(1)}, u32[]{:S(2)}, u32[]{:S(2)}) async-start(bf16[8,304,128]{2,1,0:T(8,128)(2,1)} %combine.2), calls=%async_computation.5 | async-start | bytes 1245184 | tf_op jit(solution)/shard_map/all_to_all | solution.py:478
  229.6 3.3 %collective-permute-start.7 = (bf16[256,128]{1,0:T(8,128)(2,1)S(1)}, bf16[256,128]{1,0:T(8,128)(2,1)S(1)}, u32[]{:S(2)}, u32[]{:S(2)}) collective-permute-start(bf16[256,128]{1,0:T(8,128)(2,1)S(1)} %get-tuple-element.76.gagg_own), channel_id=1, source_target_pairs={{0,1},{1,0},{2,3},{3,2},{4,5},{5,4},{6,7},{7,6},{8,9},{9,8},{10,11... | collective-permute-start | bytes 196616 | tf_op jit(solution)/shard_map/ppermute | solution.py:400
  231.7 1.2 collective-permute-start.8
  274.8 24.1 %copy-start.10 = (f32[256,128]{1,0:T(8,128)S(1)}, f32[256,128]{1,0:T(8,128)}, u32[]{:S(2)}) copy-start(f32[256,128]{1,0:T(8,128)} %copy-done.9) | copy-start | bytes 393220
  277.0 21.9 %all-to-all-start.7 = ((bf16[8,304,128]{2,1,0:T(8,128)(2,1)}), bf16[8,304,128]{2,1,0:T(8,128)(2,1)S(1)}, u32[]{:S(2)}, u32[]{:S(2)}) async-start(bf16[8,304,128]{2,1,0:T(8,128)(2,1)} %get-tuple-element.79), calls=%async_computation.7 | async-start | bytes 1245184 | tf_op jit(solution)/shard_map/all_to_all | solution.py:478
  280.6 2.8 collective-permute-start.5
  299.0 3.9 %collective-permute-start.10 = (f32[48,128]{1,0:T(8,128)S(1)}, f32[48,128]{1,0:T(8,128)S(1)}, u32[]{:S(2)}, u32[]{:S(2)}) collective-permute-start(f32[48,128]{1,0:T(8,128)S(1)} %get-tuple-element.82), channel_id=1, source_target_pairs={{0,1},{1,0},{2,3},{3,2},{4,5},{5,4},{6,7},{7,6},{8,9},{9,8},{10,11... | collective-permute-start | bytes 73736 | tf_op jit(solution)/shard_map/ppermute | solution.py:400
  302.8 7.0 %collective-permute-start.9 = (f32[256,128]{1,0:T(8,128)S(1)}, f32[256,128]{1,0:T(8,128)S(1)}, u32[]{:S(2)}, u32[]{:S(2)}) collective-permute-start(f32[256,128]{1,0:T(8,128)S(1)} %get-tuple-element.81), channel_id=1, source_target_pairs={{0,1},{1,0},{2,3},{3,2},{4,5},{5,4},{6,7},{7,6},{8,9},{9,8},{10,11... | collective-permute-start | bytes 393224 | tf_op jit(solution)/shard_map/ppermute | solution.py:400
  303.7 12.9 %all-to-all-start.8 = ((f32[16,48,128]{2,1,0:T(8,128)}), f32[16,48,128]{2,1,0:T(8,128)S(1)}, u32[]{:S(2)}, u32[]{:S(2)}) async-start(f32[16,48,128]{2,1,0:T(8,128)} %broadcast_in_dim.8), calls=%async_computation.8 | async-start | bytes 786432 | tf_op jit(solution)/shard_map/all_to_all | solution.py:373
  (11 other events, 17.0 us)
where the time goes:
time: 322 us
  blocking collectives  94.3 us (29%)
  waiting for transfers between devices  83.5 us (26%)
  starting transfers between devices  45.9 us (14%)
  Pallas kernels  43.7 us (14%)
  local copies, waits for them, and re-layouts  39.6 us (12%)
  matrix products  8.05 us (3%)
  other arithmetic  4.96 us (2%)
    all_to_all x2, blocking collectives, body(): arrived = lax.all_to_all(sent, ('x', 'y'), 0, 0, tiled=True)  74 us
    all_to_all x2, waiting for transfers between devices, body(): parts = lax.all_to_all(combined, 'z', 0, 0, tiled=True)  33.9 us
    dot_general x5, local copies, waits for them, and re-layouts, relation_table(): flat_rows = jnp.dot(query_vec, proj.astype(F32), precision=EXACT_MATMUL)  22.7 us
    all_to_all x1, blocking collectives, column_of(): return lax.all_to_all(copies, 'z', 0, 0, tiled=True)  20.4 us
    all_to_all x1, waiting for transfers between devices, column_of(): return lax.all_to_all(copies, 'z', 0, 0, tiled=True)  17.1 us
    ppermute x11, starting transfers between devices, swap(): return lax.ppermute(value, 'c', SWAP)  15.9 us
    all_to_all x2, waiting for transfers between devices, body(): rec_own = lax.all_to_all(outgoing, ('x', 'y'), 0, 0, tiled=True)  15.6 us
    pallas_call x2, Pallas kernels, forward(): pl.pallas_call(functools.partial(forward_kernel, last, tiles), out_shape=...  13.9 us
  transfers between devices with their start and end apart: 17, of which 11 were waited for; matrix products, arithmetic and copies ran while one was open for 12% of the time, Pallas kernels for 3%

commit v1 on v0

--- a/solution.py
+++ b/solution.py
@@ -28,6 +28,9 @@
 SMEM_SPEC = pl.BlockSpec(memory_space=pltpu.SMEM)
 VMEM_SPEC = pl.BlockSpec(memory_space=pltpu.VMEM)
 ANY_SPEC = pl.BlockSpec(memory_space=pl.ANY)
+HBM_SPEC = pl.BlockSpec(memory_space=pltpu.HBM)
+WIDE = R8 * H
+RM = BLK // H
 
 
 def grid_dims(node_count):
@@ -46,23 +49,59 @@
     return jnp.dot(picked, rel_table, precision=EXACT_MATMUL)
 
 
+def lanes_of(shape):
+    return lax.broadcasted_iota(jnp.int32, shape, 1) // H
+
+
+def table_kernel(flat, table, rows):
+    for j in range(R8 // RM):
+        rows[:, j, :] = flat[:, j * BLK : (j + 1) * BLK]
+    lane = lanes_of(rows.shape[1:])
+    for m in range(RM):
+        made = jnp.zeros(rows.shape[1:], F32)
+        for q in range(Q):
+            made = jnp.where(lane == q, pltpu.roll(rows[q], (q - m) * H % COLS, 1), made)
+        table[pl.ds(m, R8 // RM, stride=RM), :] = made[: R8 // RM]
+
+
+def flat_kernel(table, flat, rows):
+    lane = lanes_of(rows.shape[1:])
+    count = rows.shape[1]
+    for q in range(Q):
+        rows[q] = jnp.zeros((count, COLS), F32)
+    for m in range(RM):
+        read = table[pl.ds(m, count, stride=RM), :]
+        for q in range(Q):
+            rows[q] = jnp.where(lane == m, pltpu.roll(read, (m - q) * H % COLS, 1), rows[q])
+    for j in range(R8 // RM):
+        flat[:, j * BLK : (j + 1) * BLK] = rows[:, j, :]
+
+
+def relayout(kernel, shape, value):
+    return pl.pallas_call(
+        kernel,
+        out_shape=jax.ShapeDtypeStruct(shape, F32),
+        in_specs=[VMEM_SPEC],
+        out_specs=VMEM_SPEC,
+        scratch_shapes=[pltpu.VMEM((Q, -(-R8 // (8 * RM)) * 8, COLS), F32)],
+        compiler_params=params(),
+        cost_estimate=pl.CostEstimate(flops=0, bytes_accessed=4 << 20, transcendentals=0),
+        name=kernel.__name__,
+    )(value)
+
+
 def relation_table(query_vec, proj):
-    flat_rows = jnp.dot(query_vec, proj.astype(F32), precision=EXACT_MATMUL)
-    table = flat_rows.reshape(Q, R, H).transpose(1, 0, 2).reshape(R, COLS)
-    return jnp.pad(table, ((0, R8 - R), (0, 0)))
-
-
-def split_kernel(pos, w_ref, f_keep, f_send, b_keep, b_send):
+    flat = jnp.dot(query_vec, proj.astype(F32), precision=EXACT_MATMUL)
+    return relayout(table_kernel, (R8, COLS), jnp.pad(flat, ((0, 0), (0, WIDE - R * H))))
+
+
+def split_kernel(pos, w_ref, keep, send):
     core = pos[3]
-    own = pl.multiple_of(core * HB, HB)
-    other = pl.multiple_of((1 - core) * HB, HB)
-    f_keep[...] = w_ref[:, pl.ds(own, HB), :]
-    f_send[...] = w_ref[:, pl.ds(other, HB), :]
     for t in range(w_ref.shape[0]):
         flipped = w_ref[t].T
         low, high = flipped[:HB], flipped[HB:]
-        b_keep[t] = jnp.where(core == 0, low, high)
-        b_send[t] = jnp.where(core == 0, high, low)
+        keep[t] = jnp.where(core == 0, low, high)
+        send[t] = jnp.where(core == 0, high, low)
 
 
 def split_weights(pos, weights):
@@ -71,37 +110,44 @@
     spec = pl.BlockSpec((GROUP, HB, BLK), lambda g: (g, 0, 0))
     return pl.pallas_call(
         split_kernel,
-        out_shape=(half,) * 4,
+        out_shape=(half,) * 2,
         grid=(tiles // GROUP,),
         in_specs=[SMEM_SPEC, pl.BlockSpec((GROUP, BLK, BLK), lambda g: (g, 0, 0))],
-        out_specs=[spec] * 4,
+        out_specs=[spec] * 2,
         compiler_params=params(),
         cost_estimate=pl.CostEstimate(
-            flops=0, bytes_accessed=tiles * BLK * BLK * 2 * 3, transcendentals=0
+            flops=0, bytes_accessed=tiles * BLK * BLK * 2 * 2, transcendentals=0
         ),
         name="split_weights",
     )(pos, weights)
 
 
-def provide_kernel(dims, pos, sends, column, out):
+def provide_kernel(dims, pos, sends, column, out, blocks, sems):
     nx, nz, ny = dims
     z = pos[1]
     nodes = nx * nz * ny
-    for owner in range(nz):
-        for d in range(nx * ny):
-            reader = (d // ny) * (nz * ny) + z * ny + d % ny
+    copies = []
+    for d in range(nx * ny):
+        reader = (d // ny) * (nz * ny) + z * ny + d % ny
+        for owner in range(nz):
             block = sends[owner * nodes + reader]
             start = pl.multiple_of(block * HB, HB)
-            out[d, owner] = column[owner, pl.ds(start, HB), :]
+            blocks[d, owner] = column[owner, pl.ds(start, HB), :]
+        copies.append(pltpu.make_async_copy(blocks.at[d], out.at[d], sems.at[d]))
+        copies[-1].start()
+    for copy in copies:
+        copy.wait()
 
 
 def provide(dims, pos, sends, column):
     nx, nz, ny = dims
+    shape = (nx * ny, nz, HB, COLS)
     return pl.pallas_call(
         functools.partial(provide_kernel, dims),
-        out_shape=jax.ShapeDtypeStruct((nx * ny, nz, HB, COLS), BF16),
+        out_shape=pltpu.HBM(shape, BF16),
         in_specs=[SMEM_SPEC, SMEM_SPEC, VMEM_SPEC],
-        out_specs=VMEM_SPEC,
+        out_specs=HBM_SPEC,
+        scratch_shapes=[pltpu.VMEM(shape, BF16), pltpu.SemaphoreType.DMA((nx * ny,))],
         compiler_params=params(),
         name="provide",
     )(pos, sends, column)
@@ -116,7 +162,7 @@
             @pl.when(g < live)
             def _(source=source, g=g):
                 pltpu.make_async_copy(
-                    weights[source].at[pl.ds(g * GROUP, GROUP)],
+                    weights[source](pl.ds(g * GROUP, GROUP)),
                     buffer.at[source * groups + g],
                     sems.at[source * groups + g],
                 ).start()
@@ -131,7 +177,7 @@
         def one_group(g, carry, source=source, base=base):
             place = source * groups + g
             pltpu.make_async_copy(
-                weights[source].at[pl.ds(g * GROUP, GROUP)],
+                weights[source](pl.ds(g * GROUP, GROUP)),
                 buffer.at[place],
                 sems.at[place],
             ).wait()
@@ -172,7 +218,7 @@
         cotangent, upd_t, block_mask = refs[:3]
         next_ref, gagg_ref, upd_ref, rec, buffer, acc, w_sems, r_sems = refs[3:]
     else:
-        next_ref, agg_ref, pre_ref, rec, buffer, acc, w_sems, r_sems = refs
+        next_ref, aux_ref, rec, buffer, acc, w_sems, r_sems, aux = refs
     own = pl.multiple_of(pos[3] * HB, HB)
     other = pl.multiple_of((1 - pos[3]) * HB, HB)
     copies = [
@@ -181,7 +227,8 @@
     ]
     for copy in copies:
         copy.start()
-    start_weights(meta, tiles, (w_own, w_other), buffer, w_sems)
+    weights = [lambda g, w=w: w.at[g, pl.ds(own, HB), :] for w in (w_own, w_other)]
+    start_weights(meta, tiles, weights, buffer, w_sems)
     acc[...] = jnp.zeros_like(acc)
     for copy in copies:
         copy.wait()
@@ -190,7 +237,7 @@
         message = jnp.dot(weight, rec[slot], preferred_element_type=F32)
         acc[dst] = acc[dst] + message * table[pl.ds(rel, 1), :]
 
-    over_tiles(meta, tiles, (w_own, w_other), buffer, w_sems, one_tile)
+    over_tiles(meta, tiles, weights, buffer, w_sems, one_tile)
     aggregate = acc[...].reshape(ROWS, COLS) + bound[...]
     pre = jnp.dot(aggregate, upd[...], precision=EXACT_MATMUL, preferred_element_type=F32)
     next_ref[...] = (state[...].astype(F32) + pre * jax.nn.sigmoid(pre)).astype(BF16)
@@ -200,31 +247,35 @@
             gagg_ref, upd_ref,
         )
     else:
-        agg_ref[...] = aggregate
-        pre_ref[...] = pre
+        aux[0] = aggregate
+        aux[1] = pre
+        kept = pltpu.make_async_copy(aux, aux_ref, r_sems.at[2])
+        kept.start()
+        kept.wait()
 
 
 def forward(last, meta, pos, rec_own, rec_other, w_own, w_other, table, bound, upd, state, more):
     slots, tiles = rec_own.shape[0], w_own.shape[0]
     places = 2 * (tiles // GROUP)
     rows16 = jax.ShapeDtypeStruct((ROWS, COLS), BF16)
-    rows32 = jax.ShapeDtypeStruct((ROWS, COLS), F32)
+    pair = pltpu.HBM((2, ROWS, COLS), F32)
     if last:
         outs = (rows16, rows16, jax.ShapeDtypeStruct((H, COLS), F32))
     else:
-        outs = (rows16, rows32, rows32)
+        outs = (rows16, pair)
     return pl.pallas_call(
         functools.partial(forward_kernel, last, tiles),
         out_shape=outs,
         in_specs=[SMEM_SPEC, SMEM_SPEC] + [ANY_SPEC] * 4 + [VMEM_SPEC] * (4 + len(more)),
-        out_specs=(VMEM_SPEC,) * 3,
+        out_specs=(VMEM_SPEC,) * 3 if last else (VMEM_SPEC, HBM_SPEC),
         scratch_shapes=[
             pltpu.VMEM((slots, BLK, COLS), BF16),
             pltpu.VMEM((places, GROUP, HB, BLK), BF16),
             pltpu.VMEM((NB_DEV, HB, COLS), F32),
             pltpu.SemaphoreType.DMA((places,)),
-            pltpu.SemaphoreType.DMA((2,)),
-        ],
+            pltpu.SemaphoreType.DMA((3,)),
+        ]
+        + ([] if last else [pltpu.VMEM((2, ROWS, COLS), F32)]),
         compiler_params=params(),
         name="forward_last" if last else "forward_first",
     )(meta, pos, rec_own, rec_other, w_own, w_other, table, bound, upd, state, *more)
@@ -237,7 +288,8 @@
     nx, nz, ny = dims
     copy = pltpu.make_async_copy(rec_own, rec, r_sem.at[0])
     copy.start()
-    start_weights(meta, tiles, (w_own, w_other), buffer, w_sems)
+    weights = (lambda g: w_own.at[g], lambda g: w_other.at[g])
+    start_weights(meta, tiles, weights, buffer, w_sems)
     own = pl.multiple_of(pos[3] * HB, HB)
     other = pl.multiple_of((1 - pos[3]) * HB, HB)
     gagg[:, pl.ds(own, HB), :] = gagg_own[...].reshape(NB_DEV, HB, COLS)
@@ -259,7 +311,7 @@
         terms = jnp.sum(back * rec[slot].astype(F32), axis=0, keepdims=True)
         rel_acc[row, :] = rel_acc[row, :] + terms
 
-    over_tiles(meta, tiles, (w_own, w_other), buffer, w_sems, one_tile)
+    over_tiles(meta, tiles, weights, buffer, w_sems, one_tile)
 
     def put(d, carry):
         out[d, : nz * HB, :] = slot_acc[pl.ds(d * nz, nz)].reshape(nz * HB, COLS).astype(BF16)
@@ -337,15 +389,18 @@
 
 
 def collect_kernel(more, parts, *refs):
+    if more:
+        aux_hbm, upd_t, block_mask, aux, sem = refs[1], refs[2], refs[3], refs[-2], refs[-1]
+        copy = pltpu.make_async_copy(aux_hbm, aux, sem.at[0])
+        copy.start()
     total = parts[0].astype(F32)
     for k in range(1, parts.shape[0]):
         total = total + parts[k].astype(F32)
     grad = refs[0][...].astype(F32) + total[:ROWS]
     if more:
-        pre, aggregate, upd_t, block_mask, grad_ref, rel_ref, gagg_ref, upd_ref = refs[1:]
-        before_backward(
-            grad, pre[...], aggregate[...], upd_t[...], block_mask[...], gagg_ref, upd_ref
-        )
+        grad_ref, rel_ref, gagg_ref, upd_ref = refs[4:-2]
+        copy.wait()
+        before_backward(grad, aux[1], aux[0], upd_t[...], block_mask[...], gagg_ref, upd_ref)
     else:
         grad_ref, rel_ref = refs[1:]
     grad_ref[...] = grad
@@ -354,14 +409,19 @@
 
 def collect(chunk, parts, grad, more):
     outs = [jax.ShapeDtypeStruct((ROWS, COLS), F32), jax.ShapeDtypeStruct((chunk, COLS), F32)]
+    in_specs = [VMEM_SPEC, VMEM_SPEC]
+    scratch = []
     if more:
         outs.append(jax.ShapeDtypeStruct((ROWS, COLS), BF16))
         outs.append(jax.ShapeDtypeStruct((H, COLS), F32))
+        in_specs += [HBM_SPEC, VMEM_SPEC, VMEM_SPEC]
+        scratch = [pltpu.VMEM((2, ROWS, COLS), F32), pltpu.SemaphoreType.DMA((1,))]
     return pl.pallas_call(
         functools.partial(collect_kernel, bool(more)),
         out_shape=tuple(outs),
-        in_specs=[VMEM_SPEC] * (2 + len(more)),
+        in_specs=in_specs,
         out_specs=(VMEM_SPEC,) * len(outs),
+        scratch_shapes=scratch,
         compiler_params=params(),
         name="collect_more" if more else "collect_last",
     )(parts, grad, *more)
@@ -372,6 +432,16 @@
     copies = jnp.broadcast_to(rel[None], (count,) + rel.shape)
     parts = lax.all_to_all(copies, ("x", "y"), 0, 0, tiled=True)
     return parts.reshape(count * rel.shape[0], COLS)
+
+
+def project(query_vec, relation, scale_factor):
+    flat = relayout(flat_kernel, (Q, WIDE), relation)
+    product = jnp.dot(query_vec.T, flat, precision=EXACT_MATMUL)
+    return (product[:, : R * H] * scale_factor).astype(BF16)
+
+
+def update_sum(relation, scale_factor):
+    return relation[R8 : R8 + H].reshape(H, Q, H).sum(1) * scale_factor
 
 
 def whole_rows(core, own, other):
@@ -399,13 +469,15 @@
     def swap(value):
         return lax.ppermute(value, "c", SWAP)
 
-    def column_of(rows):
-        copies = jnp.broadcast_to(rows[None], (nz,) + rows.shape)
+    def column_of(copies):
         return lax.all_to_all(copies, "z", 0, 0, tiled=True)
+
+    def spread(rows):
+        return jnp.broadcast_to(rows[None], (nz,) + rows.shape)
 
     state = own_half(node_state)
     listed = jnp.pad(send_list.astype(BF16), ((0, 15), (0, COLS - nodes)))
-    column = column_of(jnp.concatenate([state, listed]))
+    column = column_of(spread(jnp.concatenate([state, listed])))
 
     slot = tile_slot[0, 0]
     slot = ((slot // (nz * ny)) * ny + slot % ny) * nz + (slot // ny) % nz
@@ -418,15 +490,17 @@
     upd = [jnp.tile(upd_weight[l], (Q, Q)) * block_mask for l in range(L)]
     upd_t = [u.T for u in upd]
     cot = own_half(cotangent)
-    column, meta, upd, upd_t, block_mask, cot = lax.optimization_barrier(
-        (column, meta, upd, upd_t, block_mask, cot)
-    )
+    query_vec = query_vectors(rel_table, query_rel)
+    first_table = relation_table(query_vec, rel_proj[0])
+    weights = tile_weight[0, 0]
+    f_other = swap(weights)
+    held = (column, meta, upd, upd_t, block_mask, cot, first_table, f_other)
+    held = lax.optimization_barrier(held)
+    column, meta, upd, upd_t, block_mask, cot, first_table, f_other = held
     sends = column[:, ROWS, :nodes].astype(jnp.int32).reshape(-1)
     outgoing = provide(dims, pos, sends, column)
-    outgoing, later, query_rel = lax.optimization_barrier((outgoing, pos, query_rel))
-    f_own, f_send, b_own, b_send = split_weights(later, tile_weight[0, 0])
-    f_other, b_other = swap(f_send), swap(b_send)
-    query_vec = query_vectors(rel_table, query_rel)
+    outgoing, later = lax.optimization_barrier((outgoing, pos))
+    b_own, b_send = split_weights(later, weights)
     row_ids = node * (NB_DEV * BLK) + (
         jnp.arange(NB_DEV, dtype=jnp.int32)[:, None] * BLK
         + core * HB
@@ -438,36 +512,41 @@
     received, tables = [], []
     for l in range(L):
         if l:
-            outgoing = provide(dims, pos, sends, column_of(state))
+            column, b_other = lax.optimization_barrier((column_of(spread(state)), b_other))
+            outgoing = provide(dims, pos, sends, column)
             outgoing, vectors = lax.optimization_barrier((outgoing, query_vec))
         else:
-            vectors = query_vec
+            table = first_table
         rec_own = lax.all_to_all(outgoing, ("x", "y"), 0, 0, tiled=True)
-        table = relation_table(vectors, rel_proj[l])
         if l:
+            table = relation_table(vectors, rel_proj[l])
             rec_own, table = lax.optimization_barrier((rec_own, table))
         else:
-            rec_own, table, bound, f_own, f_other, b_own, b_other = lax.optimization_barrier(
-                (rec_own, table, bound, f_own, f_other, b_own, b_other)
+            rec_own, bound, b_own, b_send = lax.optimization_barrier(
+                (rec_own, bound, b_own, b_send)
             )
         tables.append(table)
         rec_own = rec_own.reshape(nodes, HB, COLS)
         received.append(rec_own)
         last = l == L - 1
         more = (cot, upd_t[l], block_mask) if last else ()
+        rec_other = swap(rec_own)
+        if l == 0:
+            rec_other, b_send = lax.optimization_barrier((rec_other, b_send))
+            b_other = swap(b_send)
         made = forward(
-            last, meta, pos, rec_own, swap(rec_own), f_own, f_other, tables[l], bound, upd[l],
+            last, meta, pos, rec_own, rec_other, weights, f_other, tables[l], bound, upd[l],
             state, more,
         )
         state = made[0]
         if last:
             gagg, upd_sum = made[1:]
         else:
-            agg0, pre0 = made[1:]
+            aux = pltpu.with_memory_space_constraint(made[1], pltpu.HBM)
 
     grad = cot
     passed = ()
-    relations = [None] * L
+    scale_factor = float(nodes * NB_DEV * BLK) ** (-0.5)
     for l in reversed(range(L)):
         sent = backward(
             dims, chunk, meta, pos, received[l], b_own, b_other, gagg, swap(gagg), tables[l],
@@ -476,38 +555,28 @@
         arrived = lax.all_to_all(sent, ("x", "y"), 0, 0, tiled=True)
         combined, *whole = combine(dims, chunk, pos, sends, arrived)
         parts = lax.all_to_all(combined, "z", 0, 0, tiled=True)
-        more = (pre0, agg0, upd_t[0], block_mask) if l else ()
+        if whole:
+            relation = whole[0] + swap(whole[0])
+            last_proj = project(query_vec, relation, scale_factor)
+            last_upd = update_sum(relation, scale_factor)
+            parts, last_proj, last_upd = lax.optimization_barrier((parts, last_proj, last_upd))
+        more = (aux, upd_t[0], block_mask) if l else ()
         made = collect(chunk, parts, grad, more)
         grad, rel = made[:2]
         if l:
             gagg, upd_sum = made[2:]
-        rel = rel + swap(rel)
         passed = (rel,) if l else ()
-        if whole:
-            relations[l + 1] = whole[0]
-    relations[0] = gather_relations(dims, rel)
-
-    scale_factor = float(nodes * NB_DEV * BLK) ** (-0.5)
-    projs = []
-    upds = []
-    for l in range(L):
-        projs.append(
-            jnp.einsum(
-                "qh,rqk->hrk",
-                query_vec,
-                relations[l][:R].reshape(R, Q, H),
-                precision=EXACT_MATMUL,
-            ).reshape(H, R * H)
-            * scale_factor
-        )
-        upds.append(relations[l][R8 : R8 + H].reshape(H, Q, H).sum(1))
+    relation = gather_relations(dims, rel + swap(rel))
+
+    proj = jnp.stack([project(query_vec, relation, scale_factor), last_proj])
+    upds = jnp.stack([update_sum(relation, scale_factor), last_upd])
     final_state = whole_rows(core, state, swap(state))
     grad_state = whole_rows(core, grad, swap(grad))
     return (
         final_state,
         grad_state,
-        jnp.stack(projs).astype(BF16),
-        jnp.stack(upds) * scale_factor,
+        proj,
+        upds,
     )
 
 

time: 322 us -> 316 us (0.981)
  local copies, waits for them, and re-layouts: 39.6 us -> 8.16 us
  waiting for transfers between devices: 83.5 us -> 105 us
    all_to_all x2, waiting for transfers between devices: 15.6 us -> 44 us  [body(): rec_own = lax.all_to_all(outgoing, ('x', 'y'), 0, 0, tiled=True)]
    dot_general x9 -> x0, local copies, waits for them, and re-layouts: 24.1 us -> none  [the longest x5 22.7 us: relation_table(): flat_rows = jnp.dot(query_vec, proj.astype(F32), precision=EXACT_MATMUL)]
    unnamed x36 -> x18, local copies, waits for them, and re-layouts: 8.1 us -> 1.76 us
    all_to_all x2, waiting for transfers between devices: 33.9 us -> 29.1 us  [body(): parts = lax.all_to_all(combined, 'z', 0, 0, tiled=True)]
    all_to_all x1, waiting for transfers between devices: 17.1 us -> 12.9 us  [column_of(): return lax.all_to_all(copies, 'z', 0, 0, tiled=True)]
    pallas_call x3 -> x7, Pallas kernels: 12.3 us -> 15.5 us  [the longest x1 9.52 us: split_weights(): pl.pallas_call(split_kernel, out_shape=(half,) * 2, grid=(tiles // GROUP,...]
  transfers between devices with their start and end apart: 17 -> 17, of which waited for: 11 -> 12; matrix products, arithmetic and copies ran while one was open for 12% -> 5% of each run, Pallas kernels for 3% -> 5%
where the time goes in v1:
time: 316 us; the launch traced here: 315 us
  waiting for transfers between devices  105 us (33%)
  blocking collectives  94 us (30%)
  starting transfers between devices  47.2 us (15%)
  Pallas kernels  45.7 us (14%)
  local copies, waits for them, and re-layouts  8.16 us (3%)
  other arithmetic  6.63 us (2%)
  matrix products  6.45 us (2%)
    all_to_all x2, blocking collectives, body(): arrived = lax.all_to_all(sent, ('x', 'y'), 0, 0, tiled=True)  73.4 us
    all_to_all x2, waiting for transfers between devices, body(): rec_own = lax.all_to_all(outgoing, ('x', 'y'), 0, 0, tiled=True)  44 us
    all_to_all x2, waiting for transfers between devices, body(): parts = lax.all_to_all(combined, 'z', 0, 0, tiled=True)  29.1 us
    all_to_all x1, blocking collectives, column_of(): return lax.all_to_all(copies, 'z', 0, 0, tiled=True)  20.5 us
    ppermute x11, starting transfers between devices, swap(): return lax.ppermute(value, 'c', SWAP)  17.6 us
    pallas_call x2, Pallas kernels, forward(): pl.pallas_call(functools.partial(forward_kernel, last, tiles), out_shape=...  13.2 us
    all_to_all x1, waiting for transfers between devices, column_of(): return lax.all_to_all(copies, 'z', 0, 0, tiled=True)  12.9 us
    all_to_all x2, starting transfers between devices, body(): rec_own = lax.all_to_all(outgoing, ('x', 'y'), 0, 0, tiled=True)  11.8 us
  transfers between devices with their start and end apart: 17, of which 12 were waited for; matrix products, arithmetic and copies ran while one was open for 5% of the time, Pallas kernels for 5%

profile of v1, /device:TPU:1, one launch (start us, length us, event | category | flops | bytes accessed | tf_op | source)
XLA Modules:
  0.0 315.2 jit_solution(16310107535591858208)
XLA Ops:
  0.7 3.3 %collective-permute-start.1 = (bf16[192,128,128]{2,1,0:T(8,128)(2,1)}, bf16[192,128,128]{2,1,0:T(8,128)(2,1)}, u32[]{:S(2)}, u32[]{:S(2)}) collective-permute-start(bf16[192,128,128]{2,1,0:T(8,128)(2,1)} %bitcast.88), channel_id=1, source_target_pairs={{0,1},{1,0},{2,3},{3,2},{4,5},{5,4},{6,7},{7,6},{8,9},{9,8},{10,11... | collective-permute-start | bytes 18874376 | tf_op jit(solution)/shard_map/ppermute | solution.py:470
  8.0 6.6 %all-to-all-start = ((bf16[8,272,128]{2,1,0:T(8,128)(2,1)}), bf16[8,272,128]{2,1,0:T(8,128)(2,1)S(1)}, u32[]{:S(2)}, u32[]{:S(2)}) async-start(bf16[8,272,128]{2,1,0:T(8,128)(2,1)} %broadcast_in_dim.6), calls=%async_computation | async-start | bytes 1114112 | tf_op jit(solution)/shard_map/all_to_all | solution.py:473
  20.3 12.9 %all-to-all-done.column = bf16[8,272,128]{2,1,0:T(8,128)(2,1)S(1)} async-done(((bf16[8,272,128]{2,1,0:T(8,128)(2,1)}), bf16[8,272,128]{2,1,0:T(8,128)(2,1)S(1)}, u32[]{:S(2)}, u32[]{:S(2)}) %all-to-all-start) | async-done | bytes 557088 | tf_op jit(solution)/shard_map/all_to_all | solution.py:473
  35.3 6.8 %all-to-all-start.1 = ((bf16[16,8,64,128]{3,2,1,0:T(8,128)(2,1)}), bf16[16,8,64,128]{3,2,1,0:T(8,128)(2,1)S(1)}, u32[]{:S(2)}, u32[]{:S(2)}) async-start(bf16[16,8,64,128]{3,2,1,0:T(8,128)(2,1)} %provide.2), calls=%async_computation.1 | async-start | bytes 4194304 | tf_op jit(solution)/shard_map/all_to_all | solution.py:520
  42.5 9.5 %split_weights.1 = (bf16[192,64,128]{2,1,0:T(8,128)(2,1)S(1)}, bf16[192,64,128]{2,1,0:T(8,128)(2,1)}) custom-call(s32[4]{0:T(128)S(1)} %pad_add_fusion.1.pos, bf16[192,128,128]{2,1,0:T(8,128)(2,1)} %bitcast.89), custom_call_target="tpu_custom_call" | custom-call | bytes 12582912 | tf_op jit(solution)/shard_map/split_weights/pallas_call | solution.py:111
  53.8 17.3 %all-to-all-done.1 = bf16[16,8,64,128]{3,2,1,0:T(8,128)(2,1)S(1)} async-done(((bf16[16,8,64,128]{3,2,1,0:T(8,128)(2,1)}), bf16[16,8,64,128]{3,2,1,0:T(8,128)(2,1)S(1)}, u32[]{:S(2)}, u32[]{:S(2)}) %all-to-all-start.1) | async-done | bytes 2097184 | tf_op jit(solution)/shard_map/all_to_all | solution.py:520
  73.6 3.8 %collective-permute-done.2.rec_other = bf16[128,64,128]{2,1,0:T(8,128)(2,1)S(1)} collective-permute-done((bf16[128,64,128]{2,1,0:T(8,128)(2,1)S(1)}, bf16[128,64,128]{2,1,0:T(8,128)(2,1)S(1)}, u32[]{:S(2)}, u32[]{:S(2)}) %collective-permute-start.2) | collective-permute-done | bytes 2097184 | tf_op jit(solution)/shard_map/ppermute | solution.py:470
  77.7 6.0 %forward_first.1 = (bf16[256,128]{1,0:T(8,128)(2,1)S(1)}, f32[2,256,128]{2,1,0:T(8,128)}) custom-call(s32[1536]{0:T(1024)S(1)} %reshape.410.meta, s32[4]{0:T(128)S(1)} %pad_add_fusion.1.pos, bf16[128,64,128]{2,1,0:T(8,128)(2,1)S(1)} %bitcast.74, bf16[128,64,128]{2,1,0:T(8,128)(2,1)S(1)} %collective-permute-done.2.rec_other, bf16[192,128,128]{2,1,0:T(8,128)(2,1)} %bitcast.90, ...), custom_call_target="tpu_custom_call" | custom-call | tf_op jit(solution)/shard_map/forward_first/pallas_call | solution.py:266
  83.8 20.5 %all_to_all.45.column = bf16[8,256,128]{2,1,0:T(8,128)(2,1)S(1)} all-to-all(bf16[8,256,128]{2,1,0:T(8,128)(2,1)S(1)} %broadcast_in_dim.7), channel_id=1, replica_groups=mesh['x'=4,'z'=8,'y'=4,'c'=2] {'z'}, dimensions={0} | all-to-all | bytes 1048576 | tf_op jit(solution)/shard_map/all_to_all | solution.py:473
  106.4 5.0 %all-to-all-start.3 = ((bf16[16,8,64,128]{3,2,1,0:T(8,128)(2,1)}), bf16[16,8,64,128]{3,2,1,0:T(8,128)(2,1)}, u32[]{:S(2)}, u32[]{:S(2)}) async-start(bf16[16,8,64,128]{3,2,1,0:T(8,128)(2,1)} %provide.3), calls=%async_computation.3 | async-start | bytes 4194304 | tf_op jit(solution)/shard_map/all_to_all | solution.py:520
  113.8 26.8 %all-to-all-done.3 = bf16[16,8,64,128]{3,2,1,0:T(8,128)(2,1)} async-done(((bf16[16,8,64,128]{3,2,1,0:T(8,128)(2,1)}), bf16[16,8,64,128]{3,2,1,0:T(8,128)(2,1)}, u32[]{:S(2)}, u32[]{:S(2)}) %all-to-all-start.3) | async-done | bytes 2097184 | tf_op jit(solution)/shard_map/all_to_all | solution.py:520
  143.1 4.0 %collective-permute-done.4.rec_other = bf16[128,64,128]{2,1,0:T(8,128)(2,1)} collective-permute-done((bf16[128,64,128]{2,1,0:T(8,128)(2,1)}, bf16[128,64,128]{2,1,0:T(8,128)(2,1)}, u32[]{:S(2)}, u32[]{:S(2)}) %collective-permute-start.4) | collective-permute-done | bytes 2097184 | tf_op jit(solution)/shard_map/ppermute | solution.py:470
  147.2 7.2 %forward_last.1 = (bf16[256,128]{1,0:T(8,128)(2,1)S(1)}, bf16[256,128]{1,0:T(8,128)(2,1)S(1)}, f32[32,128]{1,0:T(8,128)S(1)}) custom-call(s32[1536]{0:T(1024)S(1)} %reshape.410.meta, s32[4]{0:T(128)S(1)} %pad_add_fusion.1.pos, bf16[128,64,128]{2,1,0:T(8,128)(2,1)} %bitcast.24.rec_own, bf16[128,64,128]{2,1,0:T(8,128)(2,1)} %collective-permute-done.4.rec_other, ...), custom_call_target="tpu_custom_call" | custom-call | tf_op jit(solution)/shard_map/forward_last/pallas_call | solution.py:266
  155.7 6.1 %backward.2 = bf16[16,560,128]{2,1,0:T(8,128)(2,1)S(1)} custom-call(s32[1536]{0:T(1024)S(1)} %reshape.410.meta, s32[4]{0:T(128)S(1)} %pad_add_fusion.1.pos, bf16[128,64,128]{2,1,0:T(8,128)(2,1)} %bitcast.24.rec_own, bf16[192,64,128]{2,1,0:T(8,128)(2,1)} %copy-done.1, bf16[192,64,128]{2,1,0:T(8,128)(2,1)} %collective-permute-done.3.w_other, ...), custom_call_target="tpu_custom_call" | custom-call | tf_op jit(solution)/shard_map/backward/pallas_call | solution.py:332
  161.9 37.2 %all_to_all.46.arrived = bf16[16,560,128]{2,1,0:T(8,128)(2,1)S(1)} all-to-all(bf16[16,560,128]{2,1,0:T(8,128)(2,1)S(1)} %backward.2), channel_id=1, replica_groups=mesh['x'=4,'z'=8,'y'=4,'c'=2] {'x','y'}, dimensions={0} | all-to-all | bytes 4587520 | tf_op jit(solution)/shard_map/all_to_all | solution.py:555
  201.5 3.5 %all-to-all-start.5 = ((bf16[8,304,128]{2,1,0:T(8,128)(2,1)}), bf16[8,304,128]{2,1,0:T(8,128)(2,1)S(1)}, u32[]{:S(2)}, u32[]{:S(2)}) async-start(bf16[8,304,128]{2,1,0:T(8,128)(2,1)} %combine.2), calls=%async_computation.5 | async-start | bytes 1245184 | tf_op jit(solution)/shard_map/all_to_all | solution.py:557
  205.1 17.8 %all-to-all-done.5.parts = bf16[8,304,128]{2,1,0:T(8,128)(2,1)S(1)} async-done(((bf16[8,304,128]{2,1,0:T(8,128)(2,1)}), bf16[8,304,128]{2,1,0:T(8,128)(2,1)S(1)}, u32[]{:S(2)}, u32[]{:S(2)}) %all-to-all-start.5) | async-done | bytes 622624 | tf_op jit(solution)/shard_map/all_to_all | solution.py:557
  227.9 4.9 %backward.3 = bf16[16,608,128]{2,1,0:T(8,128)(2,1)S(1)} custom-call(s32[1536]{0:T(1024)S(1)} %reshape.410.meta, s32[4]{0:T(128)S(1)} %pad_add_fusion.1.pos, bf16[128,64,128]{2,1,0:T(8,128)(2,1)S(1)} %bitcast.75, bf16[192,64,128]{2,1,0:T(8,128)(2,1)} %copy-done.1, bf16[192,64,128]{2,1,0:T(8,128)(2,1)} %collective-permute-done.3.w_other, ...), custom_call_target="tpu_custom_call" | custom-call | tf_op jit(solution)/shard_map/backward/pallas_call | solution.py:332
  232.8 36.2 %all_to_all.47.arrived = bf16[16,608,128]{2,1,0:T(8,128)(2,1)S(1)} all-to-all(bf16[16,608,128]{2,1,0:T(8,128)(2,1)S(1)} %backward.3), channel_id=1, replica_groups=mesh['x'=4,'z'=8,'y'=4,'c'=2] {'x','y'}, dimensions={0} | all-to-all | bytes 4980736 | tf_op jit(solution)/shard_map/all_to_all | solution.py:555
  271.1 3.5 %all-to-all-start.7 = ((bf16[8,304,128]{2,1,0:T(8,128)(2,1)}), bf16[8,304,128]{2,1,0:T(8,128)(2,1)S(1)}, u32[]{:S(2)}, u32[]{:S(2)}) async-start(bf16[8,304,128]{2,1,0:T(8,128)(2,1)} %get-tuple-element.80), calls=%async_computation.7 | async-start | bytes 1245184 | tf_op jit(solution)/shard_map/all_to_all | solution.py:557
  281.1 11.3 %all-to-all-done.7.parts = bf16[8,304,128]{2,1,0:T(8,128)(2,1)S(1)} async-done(((bf16[8,304,128]{2,1,0:T(8,128)(2,1)}), bf16[8,304,128]{2,1,0:T(8,128)(2,1)S(1)}, u32[]{:S(2)}, u32[]{:S(2)}) %all-to-all-start.7) | async-done | bytes 622624 | tf_op jit(solution)/shard_map/all_to_all | solution.py:557
  292.4 3.0 collective-permute-start.10
  297.0 4.2 %all-to-all-start.8 = ((f32[16,48,128]{2,1,0:T(8,128)}), f32[16,48,128]{2,1,0:T(8,128)S(1)}, u32[]{:S(2)}, u32[]{:S(2)}) async-start(f32[16,48,128]{2,1,0:T(8,128)} %broadcast_in_dim.8), calls=%async_computation.8 | async-start | bytes 786432 | tf_op jit(solution)/shard_map/all_to_all | solution.py:433
  302.7 7.8 %all-to-all-done.8 = f32[16,48,128]{2,1,0:T(8,128)S(1)} async-done(((f32[16,48,128]{2,1,0:T(8,128)}), f32[16,48,128]{2,1,0:T(8,128)S(1)}, u32[]{:S(2)}, u32[]{:S(2)}) %all-to-all-start.8) | async-done | bytes 393248 | tf_op jit(solution)/shard_map/all_to_all | solution.py:433
  (104 shorter events, 48.3 us)
Async XLA Ops:
  0.6 15.5 %copy-start.6 = (bf16[512,128]{1,0:T(8,128)(2,1)S(1)}, bf16[512,128]{1,0:T(8,128)(2,1)}, u32[]{:S(2)}) copy-start(bf16[512,128]{1,0:T(8,128)(2,1)} %param.25) | copy-start | bytes 393220
  0.7 17.2 %copy-start.7 = (s32[4]{0:T(128)S(1)}, s32[4]{0:T(128)}, u32[]{:S(2)}) copy-start(s32[4]{0:T(128)} %param.20) | copy-start | bytes 52
  0.7 18.4 %copy-start.4 = (bf16[2,32,17120]{2,1,0:T(8,128)(2,1)S(1)}, bf16[2,32,17120]{2,1,0:T(8,128)(2,1)}, u32[]{:S(2)}) copy-start(bf16[2,32,17120]{2,1,0:T(8,128)(2,1)} %param.23) | copy-start | bytes 6574084
  0.7 32.5 %collective-permute-start.1 = (bf16[192,128,128]{2,1,0:T(8,128)(2,1)}, bf16[192,128,128]{2,1,0:T(8,128)(2,1)}, u32[]{:S(2)}, u32[]{:S(2)}) collective-permute-start(bf16[192,128,128]{2,1,0:T(8,128)(2,1)} %bitcast.88), channel_id=1, source_target_pairs={{0,1},{1,0},{2,3},{3,2},{4,5},{5,4},{6,7},{7,6},{8,9},{9,8},{10,11... | collective-permute-start | bytes 18874376 | tf_op jit(solution)/shard_map/ppermute | solution.py:470
  6.2 14.0 %collective-permute-start = (s32[4,192]{1,0:T(4,128)S(1)}, s32[4,192]{1,0:T(4,128)S(1)}, u32[]{:S(2)}, u32[]{:S(2)}) collective-permute-start(s32[4,192]{1,0:T(4,128)S(1)} %add_add_fusion), channel_id=1, source_target_pairs={{0,1},{1,0},{2,3},{3,2},{4,5},{5,4},{6,7},{7,6},{8,9},{9,8},{10,11... | collective-permute-start | bytes 9224 | tf_op jit(solution)/shard_map/ppermute | solution.py:470
  8.0 9.9 %copy-start.5 = (f32[535,32]{0,1:T(8,128)S(1)}, f32[535,32]{0,1:T(8,128)}, u32[]{:S(2)}) copy-start(f32[535,32]{0,1:T(8,128)} %param.22) | copy-start | bytes 205444
  8.0 25.2 %all-to-all-start = ((bf16[8,272,128]{2,1,0:T(8,128)(2,1)}), bf16[8,272,128]{2,1,0:T(8,128)(2,1)S(1)}, u32[]{:S(2)}, u32[]{:S(2)}) async-start(bf16[8,272,128]{2,1,0:T(8,128)(2,1)} %broadcast_in_dim.6), calls=%async_computation | async-start | bytes 1114112 | tf_op jit(solution)/shard_map/all_to_all | solution.py:473
  35.3 7.0 %copy-start.8 = (s32[4]{0:T(128)S(1)}, s32[4]{0:T(128)}, u32[]{:S(2)}) copy-start(s32[4]{0:T(128)} %param.21) | copy-start | bytes 52
  35.3 35.7 %all-to-all-start.1 = ((bf16[16,8,64,128]{3,2,1,0:T(8,128)(2,1)}), bf16[16,8,64,128]{3,2,1,0:T(8,128)(2,1)S(1)}, u32[]{:S(2)}, u32[]{:S(2)}) async-start(bf16[16,8,64,128]{3,2,1,0:T(8,128)(2,1)} %provide.2), calls=%async_computation.1 | async-start | bytes 4194304 | tf_op jit(solution)/shard_map/all_to_all | solution.py:520
  71.0 6.3 %collective-permute-start.2 = (bf16[128,64,128]{2,1,0:T(8,128)(2,1)S(1)}, bf16[128,64,128]{2,1,0:T(8,128)(2,1)S(1)}, u32[]{:S(2)}, u32[]{:S(2)}) collective-permute-start(bf16[128,64,128]{2,1,0:T(8,128)(2,1)S(1)} %bitcast.73), channel_id=1, source_target_pairs={{0,1},{1,0},{2,3},{3,2},{4,5},{5,4},{6,7},{7,6},{8,9},{9,8},{10,11... | collective-permute-start | bytes 6291464 | tf_op jit(solution)/shard_map/ppermute | solution.py:470
  77.3 27.0 %collective-permute-start.3 = (bf16[192,64,128]{2,1,0:T(8,128)(2,1)}, bf16[192,64,128]{2,1,0:T(8,128)(2,1)}, u32[]{:S(2)}, u32[]{:S(2)}) collective-permute-start(bf16[192,64,128]{2,1,0:T(8,128)(2,1)} %get-tuple-element.60), channel_id=1, source_target_pairs={{0,1},{1,0},{2,3},{3,2},{4,5},{5,4},{6,7},{7,6},{8,9},{9,8},{10,11... | collective-permute-start | bytes 9437192 | tf_op jit(solution)/shard_map/ppermute | solution.py:470
  106.4 34.1 %all-to-all-start.3 = ((bf16[16,8,64,128]{3,2,1,0:T(8,128)(2,1)}), bf16[16,8,64,128]{3,2,1,0:T(8,128)(2,1)}, u32[]{:S(2)}, u32[]{:S(2)}) async-start(bf16[16,8,64,128]{3,2,1,0:T(8,128)(2,1)} %provide.3), calls=%async_computation.3 | async-start | bytes 4194304 | tf_op jit(solution)/shard_map/all_to_all | solution.py:520
  140.5 6.6 %collective-permute-start.4 = (bf16[128,64,128]{2,1,0:T(8,128)(2,1)}, bf16[128,64,128]{2,1,0:T(8,128)(2,1)}, u32[]{:S(2)}, u32[]{:S(2)}) collective-permute-start(bf16[128,64,128]{2,1,0:T(8,128)(2,1)} %bitcast.24.rec_own), channel_id=1, source_target_pairs={{0,1},{1,0},{2,3},{3,2},{4,5},{5,4},{6,7},{7,6},{8,9},{9,8},{10,11... | collective-permute-start | bytes 6291464 | tf_op jit(solution)/shard_map/ppermute | solution.py:470
  154.3 7.5 %copy-start.2 = (bf16[256,128]{1,0:T(8,128)(2,1)}, bf16[256,128]{1,0:T(8,128)(2,1)S(1)}, u32[]{:S(2)}) copy-start(bf16[256,128]{1,0:T(8,128)(2,1)S(1)} %get-tuple-element.70) | copy-start | bytes 196612
  154.4 1.3 collective-permute-start.6
  201.5 21.5 %all-to-all-start.5 = ((bf16[8,304,128]{2,1,0:T(8,128)(2,1)}), bf16[8,304,128]{2,1,0:T(8,128)(2,1)S(1)}, u32[]{:S(2)}, u32[]{:S(2)}) async-start(bf16[8,304,128]{2,1,0:T(8,128)(2,1)} %combine.2), calls=%async_computation.5 | async-start | bytes 1245184 | tf_op jit(solution)/shard_map/all_to_all | solution.py:557
  224.3 3.5 %collective-permute-start.7 = (bf16[256,128]{1,0:T(8,128)(2,1)S(1)}, bf16[256,128]{1,0:T(8,128)(2,1)S(1)}, u32[]{:S(2)}, u32[]{:S(2)}) collective-permute-start(bf16[256,128]{1,0:T(8,128)(2,1)S(1)} %get-tuple-element.77.gagg_own), channel_id=1, source_target_pairs={{0,1},{1,0},{2,3},{3,2},{4,5},{5,4},{6,7},{7,6},{8,9},{9,8},{10,11... | collective-permute-start | bytes 196616 | tf_op jit(solution)/shard_map/ppermute | solution.py:470
  269.0 8.1 %copy-start.3 = (bf16[256,128]{1,0:T(8,128)(2,1)S(1)}, bf16[256,128]{1,0:T(8,128)(2,1)}, u32[]{:S(2)}) copy-start(bf16[256,128]{1,0:T(8,128)(2,1)} %copy-done.2) | copy-start | bytes 196612
  271.1 21.2 %all-to-all-start.7 = ((bf16[8,304,128]{2,1,0:T(8,128)(2,1)}), bf16[8,304,128]{2,1,0:T(8,128)(2,1)S(1)}, u32[]{:S(2)}, u32[]{:S(2)}) async-start(bf16[8,304,128]{2,1,0:T(8,128)(2,1)} %get-tuple-element.80), calls=%async_computation.7 | async-start | bytes 1245184 | tf_op jit(solution)/shard_map/all_to_all | solution.py:557
  274.7 3.7 %collective-permute-start.8 = (f32[768,128]{1,0:T(8,128)S(1)}, f32[768,128]{1,0:T(8,128)S(1)}, u32[]{:S(2)}, u32[]{:S(2)}) collective-permute-start(f32[768,128]{1,0:T(8,128)S(1)} %get-tuple-element.81), channel_id=1, source_target_pairs={{0,1},{1,0},{2,3},{3,2},{4,5},{5,4},{6,7},{7,6},{8,9},{9,8},{10,11... | collective-permute-start | bytes 1179656 | tf_op jit(solution)/shard_map/ppermute | solution.py:470
  277.1 18.4 %collective-permute-start.5 = (bf16[256,128]{1,0:T(8,128)(2,1)S(1)}, bf16[256,128]{1,0:T(8,128)(2,1)S(1)}, u32[]{:S(2)}, u32[]{:S(2)}) collective-permute-start(bf16[256,128]{1,0:T(8,128)(2,1)S(1)} %copy-done.3), channel_id=1, source_target_pairs={{0,1},{1,0},{2,3},{3,2},{4,5},{5,4},{6,7},{7,6},{8,9},{9,8},{10,11... | collective-permute-start | bytes 196616 | tf_op jit(solution)/shard_map/ppermute | solution.py:470
  292.4 3.8 %collective-permute-start.10 = (f32[48,128]{1,0:T(8,128)S(1)}, f32[48,128]{1,0:T(8,128)S(1)}, u32[]{:S(2)}, u32[]{:S(2)}) collective-permute-start(f32[48,128]{1,0:T(8,128)S(1)} %get-tuple-element.85), channel_id=1, source_target_pairs={{0,1},{1,0},{2,3},{3,2},{4,5},{5,4},{6,7},{7,6},{8,9},{9,8},{10,11... | collective-permute-start | bytes 73736 | tf_op jit(solution)/shard_map/ppermute | solution.py:470
  295.4 6.5 %collective-permute-start.9 = (f32[256,128]{1,0:T(8,128)S(1)}, f32[256,128]{1,0:T(8,128)S(1)}, u32[]{:S(2)}, u32[]{:S(2)}) collective-permute-start(f32[256,128]{1,0:T(8,128)S(1)} %get-tuple-element.84), channel_id=1, source_target_pairs={{0,1},{1,0},{2,3},{3,2},{4,5},{5,4},{6,7},{7,6},{8,9},{9,8},{10,11... | collective-permute-start | bytes 393224 | tf_op jit(solution)/shard_map/ppermute | solution.py:470
  297.0 13.5 %all-to-all-start.8 = ((f32[16,48,128]{2,1,0:T(8,128)}), f32[16,48,128]{2,1,0:T(8,128)S(1)}, u32[]{:S(2)}, u32[]{:S(2)}) async-start(f32[16,48,128]{2,1,0:T(8,128)} %broadcast_in_dim.8), calls=%async_computation.8 | async-start | bytes 786432 | tf_op jit(solution)/shard_map/all_to_all | solution.py:433
  (2 other events, 8.1 us)

commit v2 on v1

--- a/solution.py
+++ b/solution.py
@@ -122,17 +122,18 @@
     )(pos, weights)
 
 
-def provide_kernel(dims, pos, sends, column, out, blocks, sems):
+def provide_kernel(dims, pos, sends, *refs):
     nx, nz, ny = dims
+    column, (out, blocks, sems) = refs[:nz], refs[nz:]
     z = pos[1]
     nodes = nx * nz * ny
     copies = []
     for d in range(nx * ny):
         reader = (d // ny) * (nz * ny) + z * ny + d % ny
-        for owner in range(nz):
-            block = sends[owner * nodes + reader]
+        for k in range(nz):
+            block = sends[k * nodes + reader]
             start = pl.multiple_of(block * HB, HB)
-            blocks[d, owner] = column[owner, pl.ds(start, HB), :]
+            blocks[d, lax.rem(z - k + nz, nz)] = column[k][pl.ds(start, HB), :]
         copies.append(pltpu.make_async_copy(blocks.at[d], out.at[d], sems.at[d]))
         copies[-1].start()
     for copy in copies:
@@ -145,12 +146,12 @@
     return pl.pallas_call(
         functools.partial(provide_kernel, dims),
         out_shape=pltpu.HBM(shape, BF16),
-        in_specs=[SMEM_SPEC, SMEM_SPEC, VMEM_SPEC],
+        in_specs=[SMEM_SPEC, SMEM_SPEC] + [VMEM_SPEC] * nz,
         out_specs=HBM_SPEC,
         scratch_shapes=[pltpu.VMEM(shape, BF16), pltpu.SemaphoreType.DMA((nx * ny,))],
         compiler_params=params(),
         name="provide",
-    )(pos, sends, column)
+    )(pos, sends, *column)
 
 
 def start_weights(meta, tiles, weights, buffer, sems):
@@ -360,7 +361,7 @@
     for s in range(nx * ny):
         sender = (s // ny) * (nz * ny) + z * ny + s % ny
         for owner in range(nz):
-            block = sends[owner * nodes + sender]
+            block = sends[lax.rem(z - owner + nz, nz) * nodes + sender]
             acc[owner, block] = acc[owner, block] + arrived[
                 s, owner * HB : (owner + 1) * HB, :
             ].astype(F32)
@@ -444,6 +445,10 @@
     return relation[R8 : R8 + H].reshape(H, Q, H).sum(1) * scale_factor
 
 
+def shift(value, axis, count, k):
+    return lax.ppermute(value, axis, [(s, (s + k) % count) for s in range(count)])
+
+
 def whole_rows(core, own, other):
     own, other = (v.reshape(NB_DEV, 1, HB, COLS) for v in (own, other))
     low = jnp.where(core == 0, own, other)
@@ -469,15 +474,20 @@
     def swap(value):
         return lax.ppermute(value, "c", SWAP)
 
-    def column_of(copies):
-        return lax.all_to_all(copies, "z", 0, 0, tiled=True)
-
-    def spread(rows):
-        return jnp.broadcast_to(rows[None], (nz,) + rows.shape)
+    def column_of(rows):
+        pieces = [rows] * nz
+        ahead = behind = rows
+        for k in range(1, nz // 2 + 1):
+            ahead = shift(ahead, "z", nz, 1)
+            pieces[k] = ahead
+            if k < nz - k:
+                behind = shift(behind, "z", nz, -1)
+                pieces[nz - k] = behind
+        return pieces
 
     state = own_half(node_state)
     listed = jnp.pad(send_list.astype(BF16), ((0, 15), (0, COLS - nodes)))
-    column = column_of(spread(jnp.concatenate([state, listed])))
+    column = column_of(jnp.concatenate([state, listed]))
 
     slot = tile_slot[0, 0]
     slot = ((slot // (nz * ny)) * ny + slot % ny) * nz + (slot // ny) % nz
@@ -497,7 +507,8 @@
     held = (column, meta, upd, upd_t, block_mask, cot, first_table, f_other)
     held = lax.optimization_barrier(held)
     column, meta, upd, upd_t, block_mask, cot, first_table, f_other = held
-    sends = column[:, ROWS, :nodes].astype(jnp.int32).reshape(-1)
+    sends = jnp.concatenate([p[ROWS : ROWS + 1, :nodes] for p in column])
+    sends = sends.astype(jnp.int32).reshape(-1)
     outgoing = provide(dims, pos, sends, column)
     outgoing, later = lax.optimization_barrier((outgoing, pos))
     b_own, b_send = split_weights(later, weights)
@@ -512,7 +523,7 @@
     received, tables = [], []
     for l in range(L):
         if l:
-            column, b_other = lax.optimization_barrier((column_of(spread(state)), b_other))
+            column, b_other = lax.optimization_barrier((column_of(state), b_other))
             outgoing = provide(dims, pos, sends, column)
             outgoing, vectors = lax.optimization_barrier((outgoing, query_vec))
         else:

time: 316 us -> 311 us (0.984)
  blocking collectives: 94 us -> 68 us
  starting transfers between devices: 47.2 us -> 68.3 us
  Pallas kernels: 45.7 us -> 52.2 us
  waiting for transfers between devices: 105 us -> 101 us
    all_to_all x1 -> x0, blocking collectives: 20.5 us -> none  [column_of(): return lax.all_to_all(copies, 'z', 0, 0, tiled=True)]
    ppermute x0 -> x14, starting transfers between devices: none -> 17.9 us  [shift(): lax.ppermute(value, axis, [(s, (s + k) % count) for s in range(count)])]
    ppermute x0 -> x14, waiting for transfers between devices: none -> 17.2 us  [shift(): lax.ppermute(value, axis, [(s, (s + k) % count) for s in range(count)])]
    all_to_all x1 -> x0, waiting for transfers between devices: 12.9 us -> none  [column_of(): return lax.all_to_all(copies, 'z', 0, 0, tiled=True)]
    all_to_all x2, waiting for transfers between devices: 44 us -> 35 us  [body(): rec_own = lax.all_to_all(outgoing, ('x', 'y'), 0, 0, tiled=True)]
    ppermute x11, starting transfers between devices: 17.6 us -> 25.5 us  [swap(): return lax.ppermute(value, 'c', SWAP)]
    all_to_all x1 -> x0, starting transfers between devices: 6.58 us -> none  [column_of(): return lax.all_to_all(copies, 'z', 0, 0, tiled=True)]
    all_to_all x2, blocking collectives: 73.4 us -> 68 us  [body(): arrived = lax.all_to_all(sent, ('x', 'y'), 0, 0, tiled=True)]
  transfers between devices with their start and end apart: 17 -> 30, of which waited for: 12 -> 19; matrix products, arithmetic and copies ran while one was open for 5% -> 4% of each run, Pallas kernels for 5% -> 6%
where the time goes in v2:
time: 311 us
  waiting for transfers between devices  101 us (32%)
  starting transfers between devices  68.3 us (22%)
  blocking collectives  68 us (22%)
  Pallas kernels  52.2 us (17%)
  matrix products  8.6 us (3%)
  local copies, waits for them, and re-layouts  5.99 us (2%)
  other arithmetic  5.06 us (2%)
    all_to_all x2, blocking collectives, body(): arrived = lax.all_to_all(sent, ('x', 'y'), 0, 0, tiled=True)  68 us
    all_to_all x2, waiting for transfers between devices, body(): rec_own = lax.all_to_all(outgoing, ('x', 'y'), 0, 0, tiled=True)  35 us
    all_to_all x2, waiting for transfers between devices, body(): parts = lax.all_to_all(combined, 'z', 0, 0, tiled=True)  28.9 us
    ppermute x11, starting transfers between devices, swap(): return lax.ppermute(value, 'c', SWAP)  25.5 us
    ppermute x14, starting transfers between devices, shift(): lax.ppermute(value, axis, [(s, (s + k) % count) for s in range(count)])  17.9 us
    ppermute x14, waiting for transfers between devices, shift(): lax.ppermute(value, axis, [(s, (s + k) % count) for s in range(count)])  17.2 us
    pallas_call x2, Pallas kernels, forward(): pl.pallas_call(functools.partial(forward_kernel, last, tiles), out_shape=...  16.3 us
    pallas_call x2, Pallas kernels, backward(): pl.pallas_call(functools.partial(backward_kernel, dims, tiles, chunk), ou...  14.4 us
  transfers between devices with their start and end apart: 30, of which 19 were waited for; matrix products, arithmetic and copies ran while one was open for 4% of the time, Pallas kernels for 6%

profile of v2, /device:TPU:1, one launch (start us, length us, event | category | flops | bytes accessed | tf_op | source)
XLA Modules:
  0.0 310.5 jit_solution(3303337300220202143)
XLA Ops:
  4.7 3.9 %collective-permute-start.4 = (bf16[272,128]{1,0:T(8,128)(2,1)S(1)}, bf16[272,128]{1,0:T(8,128)(2,1)S(1)}, u32[]{:S(2)}, u32[]{:S(2)}) collective-permute-start(bf16[272,128]{1,0:T(8,128)(2,1)S(1)} %fusion.12.refs_0_), channel_id=1, source_target_pairs={{0,56},{8,0},{16,8},{24,16},{32,24},{40,32},{48,40},{56,48},{1,57}... | collective-permute-start | bytes 208904 | tf_op jit(solution)/shard_map/ppermute | solution.py:449
  25.7 4.0 %collective-permute-done.3.refs_4_ = bf16[272,128]{1,0:T(8,128)(2,1)S(1)} collective-permute-done((bf16[272,128]{1,0:T(8,128)(2,1)S(1)}, bf16[272,128]{1,0:T(8,128)(2,1)S(1)}, u32[]{:S(2)}, u32[]{:S(2)}) %collective-permute-start.3) | collective-permute-done | bytes 69664 | tf_op jit(solution)/shard_map/ppermute | solution.py:449
  31.9 6.8 %all-to-all-start = ((bf16[16,8,64,128]{3,2,1,0:T(8,128)(2,1)}), bf16[16,8,64,128]{3,2,1,0:T(8,128)(2,1)S(1)}, u32[]{:S(2)}, u32[]{:S(2)}) async-start(bf16[16,8,64,128]{3,2,1,0:T(8,128)(2,1)} %provide.2), calls=%async_computation | async-start | bytes 4194304 | tf_op jit(solution)/shard_map/all_to_all | solution.py:531
  39.1 9.5 %split_weights.1 = (bf16[192,64,128]{2,1,0:T(8,128)(2,1)S(1)}, bf16[192,64,128]{2,1,0:T(8,128)(2,1)}) custom-call(s32[4]{0:T(128)S(1)} %pad_add_fusion.1.pos, bf16[192,128,128]{2,1,0:T(8,128)(2,1)} %bitcast.87), custom_call_target="tpu_custom_call" | custom-call | bytes 12582912 | tf_op jit(solution)/shard_map/split_weights/pallas_call | solution.py:111
  50.4 13.4 %all-to-all-done = bf16[16,8,64,128]{3,2,1,0:T(8,128)(2,1)S(1)} async-done(((bf16[16,8,64,128]{3,2,1,0:T(8,128)(2,1)}), bf16[16,8,64,128]{3,2,1,0:T(8,128)(2,1)S(1)}, u32[]{:S(2)}, u32[]{:S(2)}) %all-to-all-start) | async-done | bytes 2097184 | tf_op jit(solution)/shard_map/all_to_all | solution.py:531
  63.8 5.9 %collective-permute-start.9 = (bf16[128,64,128]{2,1,0:T(8,128)(2,1)S(1)}, bf16[128,64,128]{2,1,0:T(8,128)(2,1)S(1)}, u32[]{:S(2)}, u32[]{:S(2)}) collective-permute-start(bf16[128,64,128]{2,1,0:T(8,128)(2,1)S(1)} %bitcast.75), channel_id=1, source_target_pairs={{0,1},{1,0},{2,3},{3,2},{4,5},{5,4},{6,7},{7,6},{8,9},{9,8},{10,11... | collective-permute-start | bytes 6291464 | tf_op jit(solution)/shard_map/ppermute | solution.py:475
  69.7 3.8 %collective-permute-done.9.rec_other = bf16[128,64,128]{2,1,0:T(8,128)(2,1)S(1)} collective-permute-done((bf16[128,64,128]{2,1,0:T(8,128)(2,1)S(1)}, bf16[128,64,128]{2,1,0:T(8,128)(2,1)S(1)}, u32[]{:S(2)}, u32[]{:S(2)}) %collective-permute-start.9) | collective-permute-done | bytes 2097184 | tf_op jit(solution)/shard_map/ppermute | solution.py:475
  73.9 7.4 %forward_first.1 = (bf16[256,128]{1,0:T(8,128)(2,1)S(1)}, f32[2,256,128]{2,1,0:T(8,128)}) custom-call(s32[1536]{0:T(1024)S(1)} %reshape.408.meta, s32[4]{0:T(128)S(1)} %pad_add_fusion.1.pos, bf16[128,64,128]{2,1,0:T(8,128)(2,1)S(1)} %bitcast.76, bf16[128,64,128]{2,1,0:T(8,128)(2,1)S(1)} %collective-permute-done.9.rec_other, bf16[192,128,128]{2,1,0:T(8,128)(2,1)} %bitcast.88, ...), custom_call_target="tpu_custom_call" | custom-call | tf_op jit(solution)/shard_map/forward_first/pallas_call | solution.py:267
  94.8 4.3 %collective-permute-done.13.refs_4_ = bf16[256,128]{1,0:T(8,128)(2,1)S(1)} collective-permute-done((bf16[256,128]{1,0:T(8,128)(2,1)S(1)}, bf16[256,128]{1,0:T(8,128)(2,1)S(1)}, u32[]{:S(2)}, u32[]{:S(2)}) %collective-permute-start.13) | collective-permute-done | bytes 65568 | tf_op jit(solution)/shard_map/ppermute | solution.py:449
  101.2 4.5 %all-to-all-start.1 = ((bf16[16,8,64,128]{3,2,1,0:T(8,128)(2,1)}), bf16[16,8,64,128]{3,2,1,0:T(8,128)(2,1)}, u32[]{:S(2)}, u32[]{:S(2)}) async-start(bf16[16,8,64,128]{3,2,1,0:T(8,128)(2,1)} %provide.3), calls=%async_computation.1 | async-start | bytes 4194304 | tf_op jit(solution)/shard_map/all_to_all | solution.py:531
  108.0 21.5 %all-to-all-done.1 = bf16[16,8,64,128]{3,2,1,0:T(8,128)(2,1)} async-done(((bf16[16,8,64,128]{3,2,1,0:T(8,128)(2,1)}), bf16[16,8,64,128]{3,2,1,0:T(8,128)(2,1)}, u32[]{:S(2)}, u32[]{:S(2)}) %all-to-all-start.1) | async-done | bytes 2097184 | tf_op jit(solution)/shard_map/all_to_all | solution.py:531
  129.5 6.7 %collective-permute-start.18 = (bf16[128,64,128]{2,1,0:T(8,128)(2,1)}, bf16[128,64,128]{2,1,0:T(8,128)(2,1)}, u32[]{:S(2)}, u32[]{:S(2)}) collective-permute-start(bf16[128,64,128]{2,1,0:T(8,128)(2,1)} %bitcast.25.rec_own), channel_id=1, source_target_pairs={{0,1},{1,0},{2,3},{3,2},{4,5},{5,4},{6,7},{7,6},{8,9},{9,8},{10,11... | collective-permute-start | bytes 6291464 | tf_op jit(solution)/shard_map/ppermute | solution.py:475
  136.3 4.0 %collective-permute-done.18.rec_other = bf16[128,64,128]{2,1,0:T(8,128)(2,1)} collective-permute-done((bf16[128,64,128]{2,1,0:T(8,128)(2,1)}, bf16[128,64,128]{2,1,0:T(8,128)(2,1)}, u32[]{:S(2)}, u32[]{:S(2)}) %collective-permute-start.18) | collective-permute-done | bytes 2097184 | tf_op jit(solution)/shard_map/ppermute | solution.py:475
  140.3 8.9 %forward_last.1 = (bf16[256,128]{1,0:T(8,128)(2,1)S(1)}, bf16[256,128]{1,0:T(8,128)(2,1)S(1)}, f32[32,128]{1,0:T(8,128)S(1)}) custom-call(s32[1536]{0:T(1024)S(1)} %reshape.408.meta, s32[4]{0:T(128)S(1)} %pad_add_fusion.1.pos, bf16[128,64,128]{2,1,0:T(8,128)(2,1)} %bitcast.25.rec_own, bf16[128,64,128]{2,1,0:T(8,128)(2,1)} %collective-permute-done.18.rec_other, ...), custom_call_target="tpu_custom_call" | custom-call | tf_op jit(solution)/shard_map/forward_last/pallas_call | solution.py:267
  150.6 8.0 %backward.2 = bf16[16,560,128]{2,1,0:T(8,128)(2,1)S(1)} custom-call(s32[1536]{0:T(1024)S(1)} %reshape.408.meta, s32[4]{0:T(128)S(1)} %pad_add_fusion.1.pos, bf16[128,64,128]{2,1,0:T(8,128)(2,1)} %bitcast.25.rec_own, bf16[192,64,128]{2,1,0:T(8,128)(2,1)} %copy-done.1, bf16[192,64,128]{2,1,0:T(8,128)(2,1)} %collective-permute-done.17.w_other, ...), custom_call_target="tpu_custom_call" | custom-call | tf_op jit(solution)/shard_map/backward/pallas_call | solution.py:333
  158.6 33.2 %all_to_all.35.arrived = bf16[16,560,128]{2,1,0:T(8,128)(2,1)S(1)} all-to-all(bf16[16,560,128]{2,1,0:T(8,128)(2,1)S(1)} %backward.2), channel_id=1, replica_groups=mesh['x'=4,'z'=8,'y'=4,'c'=2] {'x','y'}, dimensions={0} | all-to-all | bytes 4587520 | tf_op jit(solution)/shard_map/all_to_all | solution.py:566
  194.2 5.9 %all-to-all-start.3 = ((bf16[8,304,128]{2,1,0:T(8,128)(2,1)}), bf16[8,304,128]{2,1,0:T(8,128)(2,1)S(1)}, u32[]{:S(2)}, u32[]{:S(2)}) async-start(bf16[8,304,128]{2,1,0:T(8,128)(2,1)} %combine.2), calls=%async_computation.3 | async-start | bytes 1245184 | tf_op jit(solution)/shard_map/all_to_all | solution.py:568
  200.2 17.7 %all-to-all-done.3.parts = bf16[8,304,128]{2,1,0:T(8,128)(2,1)S(1)} async-done(((bf16[8,304,128]{2,1,0:T(8,128)(2,1)}), bf16[8,304,128]{2,1,0:T(8,128)(2,1)S(1)}, u32[]{:S(2)}, u32[]{:S(2)}) %all-to-all-start.3) | async-done | bytes 622624 | tf_op jit(solution)/shard_map/all_to_all | solution.py:568
  223.1 6.4 %backward.3 = bf16[16,608,128]{2,1,0:T(8,128)(2,1)S(1)} custom-call(s32[1536]{0:T(1024)S(1)} %reshape.408.meta, s32[4]{0:T(128)S(1)} %pad_add_fusion.1.pos, bf16[128,64,128]{2,1,0:T(8,128)(2,1)S(1)} %bitcast.77, bf16[192,64,128]{2,1,0:T(8,128)(2,1)} %copy-done.1, bf16[192,64,128]{2,1,0:T(8,128)(2,1)} %collective-permute-done.17.w_other, ...), custom_call_target="tpu_custom_call" | custom-call | tf_op jit(solution)/shard_map/backward/pallas_call | solution.py:333
  229.4 34.8 %all_to_all.36.arrived = bf16[16,608,128]{2,1,0:T(8,128)(2,1)S(1)} all-to-all(bf16[16,608,128]{2,1,0:T(8,128)(2,1)S(1)} %backward.3), channel_id=1, replica_groups=mesh['x'=4,'z'=8,'y'=4,'c'=2] {'x','y'}, dimensions={0} | all-to-all | bytes 4980736 | tf_op jit(solution)/shard_map/all_to_all | solution.py:566
  266.5 3.5 %all-to-all-start.5 = ((bf16[8,304,128]{2,1,0:T(8,128)(2,1)}), bf16[8,304,128]{2,1,0:T(8,128)(2,1)S(1)}, u32[]{:S(2)}, u32[]{:S(2)}) async-start(bf16[8,304,128]{2,1,0:T(8,128)(2,1)} %get-tuple-element.108), calls=%async_computation.5 | async-start | bytes 1245184 | tf_op jit(solution)/shard_map/all_to_all | solution.py:568
  276.4 11.3 %all-to-all-done.5.parts = bf16[8,304,128]{2,1,0:T(8,128)(2,1)S(1)} async-done(((bf16[8,304,128]{2,1,0:T(8,128)(2,1)}), bf16[8,304,128]{2,1,0:T(8,128)(2,1)S(1)}, u32[]{:S(2)}, u32[]{:S(2)}) %all-to-all-start.5) | async-done | bytes 622624 | tf_op jit(solution)/shard_map/all_to_all | solution.py:568
  292.3 4.2 %all-to-all-start.6 = ((f32[16,48,128]{2,1,0:T(8,128)}), f32[16,48,128]{2,1,0:T(8,128)S(1)}, u32[]{:S(2)}, u32[]{:S(2)}) async-start(f32[16,48,128]{2,1,0:T(8,128)} %broadcast_in_dim.2), calls=%async_computation.6 | async-start | bytes 786432 | tf_op jit(solution)/shard_map/all_to_all | solution.py:434
  298.0 7.8 %all-to-all-done.6 = f32[16,48,128]{2,1,0:T(8,128)S(1)} async-done(((f32[16,48,128]{2,1,0:T(8,128)}), f32[16,48,128]{2,1,0:T(8,128)S(1)}, u32[]{:S(2)}, u32[]{:S(2)}) %all-to-all-start.6) | async-done | bytes 393248 | tf_op jit(solution)/shard_map/all_to_all | solution.py:434
  (134 shorter events, 71.3 us)
Async XLA Ops:
  0.7 29.0 %collective-permute-start.8 = (bf16[192,128,128]{2,1,0:T(8,128)(2,1)}, bf16[192,128,128]{2,1,0:T(8,128)(2,1)}, u32[]{:S(2)}, u32[]{:S(2)}) collective-permute-start(bf16[192,128,128]{2,1,0:T(8,128)(2,1)} %bitcast.86), channel_id=1, source_target_pairs={{0,1},{1,0},{2,3},{3,2},{4,5},{5,4},{6,7},{7,6},{8,9},{9,8},{10,11... | collective-permute-start | bytes 18874376 | tf_op jit(solution)/shard_map/ppermute | solution.py:475
  4.7 11.0 %collective-permute-start.4 = (bf16[272,128]{1,0:T(8,128)(2,1)S(1)}, bf16[272,128]{1,0:T(8,128)(2,1)S(1)}, u32[]{:S(2)}, u32[]{:S(2)}) collective-permute-start(bf16[272,128]{1,0:T(8,128)(2,1)S(1)} %fusion.12.refs_0_), channel_id=1, source_target_pairs={{0,56},{8,0},{16,8},{24,16},{32,24},{40,32},{48,40},{56,48},{1,57}... | collective-permute-start | bytes 208904 | tf_op jit(solution)/shard_map/ppermute | solution.py:449
  8.6 6.9 %collective-permute-start = (bf16[272,128]{1,0:T(8,128)(2,1)S(1)}, bf16[272,128]{1,0:T(8,128)(2,1)S(1)}, u32[]{:S(2)}, u32[]{:S(2)}) collective-permute-start(bf16[272,128]{1,0:T(8,128)(2,1)S(1)} %fusion.12.refs_0_), channel_id=1, source_target_pairs={{0,8},{8,16},{16,24},{24,32},{32,40},{40,48},{48,56},{56,0},{1,9},... | collective-permute-start | bytes 208904 | tf_op jit(solution)/shard_map/ppermute | solution.py:449
  10.8 14.5 %collective-permute-start.7 = (s32[4,192]{1,0:T(4,128)S(1)}, s32[4,192]{1,0:T(4,128)S(1)}, u32[]{:S(2)}, u32[]{:S(2)}) collective-permute-start(s32[4,192]{1,0:T(4,128)S(1)} %add_add_fusion), channel_id=1, source_target_pairs={{0,1},{1,0},{2,3},{3,2},{4,5},{5,4},{6,7},{7,6},{8,9},{9,8},{10,11... | collective-permute-start | bytes 9224 | tf_op jit(solution)/shard_map/ppermute | solution.py:475
  15.6 5.4 %collective-permute-start.1 = (bf16[272,128]{1,0:T(8,128)(2,1)S(1)}, bf16[272,128]{1,0:T(8,128)(2,1)S(1)}, u32[]{:S(2)}, u32[]{:S(2)}) collective-permute-start(bf16[272,128]{1,0:T(8,128)(2,1)S(1)} %collective-permute-done.refs_1_), channel_id=1, source_target_pairs={{0,8},{8,16},{16,24},{24,32},{32,40},{40,48},{48,56},{56,0},{1,9},... | collective-permute-start | bytes 208904 | tf_op jit(solution)/shard_map/ppermute | solution.py:449
  15.7 5.9 %collective-permute-start.5 = (bf16[272,128]{1,0:T(8,128)(2,1)S(1)}, bf16[272,128]{1,0:T(8,128)(2,1)S(1)}, u32[]{:S(2)}, u32[]{:S(2)}) collective-permute-start(bf16[272,128]{1,0:T(8,128)(2,1)S(1)} %collective-permute-done.4.refs_7_), channel_id=1, source_target_pairs={{0,56},{8,0},{16,8},{24,16},{32,24},{40,32},{48,40},{56,48},{1,57}... | collective-permute-start | bytes 208904 | tf_op jit(solution)/shard_map/ppermute | solution.py:449
  21.0 4.4 %collective-permute-start.2 = (bf16[272,128]{1,0:T(8,128)(2,1)S(1)}, bf16[272,128]{1,0:T(8,128)(2,1)S(1)}, u32[]{:S(2)}, u32[]{:S(2)}) collective-permute-start(bf16[272,128]{1,0:T(8,128)(2,1)S(1)} %collective-permute-done.1.refs_2_), channel_id=1, source_target_pairs={{0,8},{8,16},{16,24},{24,32},{32,40},{40,48},{48,56},{56,0},{1,9},... | collective-permute-start | bytes 208904 | tf_op jit(solution)/shard_map/ppermute | solution.py:449
  25.3 4.4 %collective-permute-start.3 = (bf16[272,128]{1,0:T(8,128)(2,1)S(1)}, bf16[272,128]{1,0:T(8,128)(2,1)S(1)}, u32[]{:S(2)}, u32[]{:S(2)}) collective-permute-start(bf16[272,128]{1,0:T(8,128)(2,1)S(1)} %collective-permute-done.2.refs_3_), channel_id=1, source_target_pairs={{0,8},{8,16},{16,24},{24,32},{32,40},{40,48},{48,56},{56,0},{1,9},... | collective-permute-start | bytes 208904 | tf_op jit(solution)/shard_map/ppermute | solution.py:449
  31.9 31.9 %all-to-all-start = ((bf16[16,8,64,128]{3,2,1,0:T(8,128)(2,1)}), bf16[16,8,64,128]{3,2,1,0:T(8,128)(2,1)S(1)}, u32[]{:S(2)}, u32[]{:S(2)}) async-start(bf16[16,8,64,128]{3,2,1,0:T(8,128)(2,1)} %provide.2), calls=%async_computation | async-start | bytes 4194304 | tf_op jit(solution)/shard_map/all_to_all | solution.py:531
  63.8 9.7 %collective-permute-start.9 = (bf16[128,64,128]{2,1,0:T(8,128)(2,1)S(1)}, bf16[128,64,128]{2,1,0:T(8,128)(2,1)S(1)}, u32[]{:S(2)}, u32[]{:S(2)}) collective-permute-start(bf16[128,64,128]{2,1,0:T(8,128)(2,1)S(1)} %bitcast.75), channel_id=1, source_target_pairs={{0,1},{1,0},{2,3},{3,2},{4,5},{5,4},{6,7},{7,6},{8,9},{9,8},{10,11... | collective-permute-start | bytes 6291464 | tf_op jit(solution)/shard_map/ppermute | solution.py:475
  73.5 25.6 %collective-permute-start.17 = (bf16[192,64,128]{2,1,0:T(8,128)(2,1)}, bf16[192,64,128]{2,1,0:T(8,128)(2,1)}, u32[]{:S(2)}, u32[]{:S(2)}) collective-permute-start(bf16[192,64,128]{2,1,0:T(8,128)(2,1)} %get-tuple-element.81), channel_id=1, source_target_pairs={{0,1},{1,0},{2,3},{3,2},{4,5},{5,4},{6,7},{7,6},{8,9},{9,8},{10,11... | collective-permute-start | bytes 9437192 | tf_op jit(solution)/shard_map/ppermute | solution.py:475
  81.3 4.8 %collective-permute-start.10 = (bf16[256,128]{1,0:T(8,128)(2,1)S(1)}, bf16[256,128]{1,0:T(8,128)(2,1)S(1)}, u32[]{:S(2)}, u32[]{:S(2)}) collective-permute-start(bf16[256,128]{1,0:T(8,128)(2,1)S(1)} %get-tuple-element.82.refs_0_.state), channel_id=1, source_target_pairs={{0,8},{8,16},{16,24},{24,32},{32,40},{40,48},{48,56},{56,0},{1,9},... | collective-permute-start | bytes 196616 | tf_op jit(solution)/shard_map/ppermute | solution.py:449
  81.4 4.7 %collective-permute-start.14 = (bf16[256,128]{1,0:T(8,128)(2,1)S(1)}, bf16[256,128]{1,0:T(8,128)(2,1)S(1)}, u32[]{:S(2)}, u32[]{:S(2)}) collective-permute-start(bf16[256,128]{1,0:T(8,128)(2,1)S(1)} %get-tuple-element.82.refs_0_.state), channel_id=1, source_target_pairs={{0,56},{8,0},{16,8},{24,16},{32,24},{40,32},{48,40},{56,48},{1,57}... | collective-permute-start | bytes 196616 | tf_op jit(solution)/shard_map/ppermute | solution.py:449
  86.1 4.3 %collective-permute-start.11 = (bf16[256,128]{1,0:T(8,128)(2,1)S(1)}, bf16[256,128]{1,0:T(8,128)(2,1)S(1)}, u32[]{:S(2)}, u32[]{:S(2)}) collective-permute-start(bf16[256,128]{1,0:T(8,128)(2,1)S(1)} %collective-permute-done.10.refs_1_), channel_id=1, source_target_pairs={{0,8},{8,16},{16,24},{24,32},{32,40},{40,48},{48,56},{56,0},{1,9},... | collective-permute-start | bytes 196616 | tf_op jit(solution)/shard_map/ppermute | solution.py:449
  86.1 4.3 %collective-permute-start.15 = (bf16[256,128]{1,0:T(8,128)(2,1)S(1)}, bf16[256,128]{1,0:T(8,128)(2,1)S(1)}, u32[]{:S(2)}, u32[]{:S(2)}) collective-permute-start(bf16[256,128]{1,0:T(8,128)(2,1)S(1)} %collective-permute-done.14.refs_7_), channel_id=1, source_target_pairs={{0,56},{8,0},{16,8},{24,16},{32,24},{40,32},{48,40},{56,48},{1,57}... | collective-permute-start | bytes 196616 | tf_op jit(solution)/shard_map/ppermute | solution.py:449
  90.4 4.3 %collective-permute-start.12 = (bf16[256,128]{1,0:T(8,128)(2,1)S(1)}, bf16[256,128]{1,0:T(8,128)(2,1)S(1)}, u32[]{:S(2)}, u32[]{:S(2)}) collective-permute-start(bf16[256,128]{1,0:T(8,128)(2,1)S(1)} %collective-permute-done.11.refs_2_), channel_id=1, source_target_pairs={{0,8},{8,16},{16,24},{24,32},{32,40},{40,48},{48,56},{56,0},{1,9},... | collective-permute-start | bytes 196616 | tf_op jit(solution)/shard_map/ppermute | solution.py:449
  90.4 4.3 %collective-permute-start.16 = (bf16[256,128]{1,0:T(8,128)(2,1)S(1)}, bf16[256,128]{1,0:T(8,128)(2,1)S(1)}, u32[]{:S(2)}, u32[]{:S(2)}) collective-permute-start(bf16[256,128]{1,0:T(8,128)(2,1)S(1)} %collective-permute-done.15.refs_6_), channel_id=1, source_target_pairs={{0,56},{8,0},{16,8},{24,16},{32,24},{40,32},{48,40},{56,48},{1,57}... | collective-permute-start | bytes 196616 | tf_op jit(solution)/shard_map/ppermute | solution.py:449
  101.2 28.3 %all-to-all-start.1 = ((bf16[16,8,64,128]{3,2,1,0:T(8,128)(2,1)}), bf16[16,8,64,128]{3,2,1,0:T(8,128)(2,1)}, u32[]{:S(2)}, u32[]{:S(2)}) async-start(bf16[16,8,64,128]{3,2,1,0:T(8,128)(2,1)} %provide.3), calls=%async_computation.1 | async-start | bytes 4194304 | tf_op jit(solution)/shard_map/all_to_all | solution.py:531
  129.5 10.8 %collective-permute-start.18 = (bf16[128,64,128]{2,1,0:T(8,128)(2,1)}, bf16[128,64,128]{2,1,0:T(8,128)(2,1)}, u32[]{:S(2)}, u32[]{:S(2)}) collective-permute-start(bf16[128,64,128]{2,1,0:T(8,128)(2,1)} %bitcast.25.rec_own), channel_id=1, source_target_pairs={{0,1},{1,0},{2,3},{3,2},{4,5},{5,4},{6,7},{7,6},{8,9},{9,8},{10,11... | collective-permute-start | bytes 6291464 | tf_op jit(solution)/shard_map/ppermute | solution.py:475
  194.2 23.7 %all-to-all-start.3 = ((bf16[8,304,128]{2,1,0:T(8,128)(2,1)}), bf16[8,304,128]{2,1,0:T(8,128)(2,1)S(1)}, u32[]{:S(2)}, u32[]{:S(2)}) async-start(bf16[8,304,128]{2,1,0:T(8,128)(2,1)} %combine.2), calls=%async_computation.3 | async-start | bytes 1245184 | tf_op jit(solution)/shard_map/all_to_all | solution.py:568
  266.5 21.2 %all-to-all-start.5 = ((bf16[8,304,128]{2,1,0:T(8,128)(2,1)}), bf16[8,304,128]{2,1,0:T(8,128)(2,1)S(1)}, u32[]{:S(2)}, u32[]{:S(2)}) async-start(bf16[8,304,128]{2,1,0:T(8,128)(2,1)} %get-tuple-element.108), calls=%async_computation.5 | async-start | bytes 1245184 | tf_op jit(solution)/shard_map/all_to_all | solution.py:568
  272.4 18.4 %collective-permute-start.19 = (bf16[256,128]{1,0:T(8,128)(2,1)S(1)}, bf16[256,128]{1,0:T(8,128)(2,1)S(1)}, u32[]{:S(2)}, u32[]{:S(2)}) collective-permute-start(bf16[256,128]{1,0:T(8,128)(2,1)S(1)} %copy-done.3), channel_id=1, source_target_pairs={{0,1},{1,0},{2,3},{3,2},{4,5},{5,4},{6,7},{7,6},{8,9},{9,8},{10,11... | collective-permute-start | bytes 196616 | tf_op jit(solution)/shard_map/ppermute | solution.py:475
  290.7 6.5 %collective-permute-start.23 = (f32[256,128]{1,0:T(8,128)S(1)}, f32[256,128]{1,0:T(8,128)S(1)}, u32[]{:S(2)}, u32[]{:S(2)}) collective-permute-start(f32[256,128]{1,0:T(8,128)S(1)} %get-tuple-element.112), channel_id=1, source_target_pairs={{0,1},{1,0},{2,3},{3,2},{4,5},{5,4},{6,7},{7,6},{8,9},{9,8},{10,11... | collective-permute-start | bytes 393224 | tf_op jit(solution)/shard_map/ppermute | solution.py:475
  292.3 13.5 %all-to-all-start.6 = ((f32[16,48,128]{2,1,0:T(8,128)}), f32[16,48,128]{2,1,0:T(8,128)S(1)}, u32[]{:S(2)}, u32[]{:S(2)}) async-start(f32[16,48,128]{2,1,0:T(8,128)} %broadcast_in_dim.2), calls=%async_computation.6 | async-start | bytes 786432 | tf_op jit(solution)/shard_map/all_to_all | solution.py:434
  (14 other events, 96.1 us)

commit v3 on v2

--- a/solution.py
+++ b/solution.py
@@ -64,17 +64,26 @@
         table[pl.ds(m, R8 // RM, stride=RM), :] = made[: R8 // RM]
 
 
-def flat_kernel(table, flat, rows):
+def project_kernel(scale_factor, query_cols, *refs):
+    relations, (out, rows) = refs[:L], refs[L:]
     lane = lanes_of(rows.shape[1:])
     count = rows.shape[1]
-    for q in range(Q):
-        rows[q] = jnp.zeros((count, COLS), F32)
-    for m in range(RM):
-        read = table[pl.ds(m, count, stride=RM), :]
+    for l in range(L):
         for q in range(Q):
-            rows[q] = jnp.where(lane == m, pltpu.roll(read, (m - q) * H % COLS, 1), rows[q])
-    for j in range(R8 // RM):
-        flat[:, j * BLK : (j + 1) * BLK] = rows[:, j, :]
+            rows[q] = jnp.zeros((count, COLS), F32)
+        for m in range(RM):
+            read = relations[l][pl.ds(m, count, stride=RM), :]
+            for q in range(Q):
+                rows[q] = jnp.where(lane == m, pltpu.roll(read, (m - q) * H % COLS, 1), rows[q])
+        cols = [
+            jnp.broadcast_to(query_cols[:, q : q + 1] * scale_factor, (H, COLS)) for q in range(Q)
+        ]
+        for j in range(R8 // RM):
+            made = cols[0] * rows[0, j : j + 1, :]
+            for q in range(1, Q):
+                made = made + cols[q] * rows[q, j : j + 1, :]
+            width = min(BLK, R * H - j * BLK)
+            out[l, :, j * BLK : j * BLK + width] = made[:, :width].astype(BF16)
 
 
 def relayout(kernel, shape, value):
@@ -435,10 +444,16 @@
     return parts.reshape(count * rel.shape[0], COLS)
 
 
-def project(query_vec, relation, scale_factor):
-    flat = relayout(flat_kernel, (Q, WIDE), relation)
-    product = jnp.dot(query_vec.T, flat, precision=EXACT_MATMUL)
-    return (product[:, : R * H] * scale_factor).astype(BF16)
+def project(query_vec, relations, scale_factor):
+    return pl.pallas_call(
+        functools.partial(project_kernel, scale_factor),
+        out_shape=jax.ShapeDtypeStruct((L, H, R * H), BF16),
+        in_specs=[VMEM_SPEC] * (1 + L),
+        out_specs=VMEM_SPEC,
+        scratch_shapes=[pltpu.VMEM((Q, -(-R8 // (8 * RM)) * 8, COLS), F32)],
+        compiler_params=params(),
+        name="project",
+    )(query_vec.T, *relations)
 
 
 def update_sum(relation, scale_factor):
@@ -500,17 +515,17 @@
     upd = [jnp.tile(upd_weight[l], (Q, Q)) * block_mask for l in range(L)]
     upd_t = [u.T for u in upd]
     cot = own_half(cotangent)
-    query_vec = query_vectors(rel_table, query_rel)
-    first_table = relation_table(query_vec, rel_proj[0])
     weights = tile_weight[0, 0]
     f_other = swap(weights)
-    held = (column, meta, upd, upd_t, block_mask, cot, first_table, f_other)
+    held = (column, meta, upd, upd_t, block_mask, cot, f_other)
     held = lax.optimization_barrier(held)
-    column, meta, upd, upd_t, block_mask, cot, first_table, f_other = held
+    column, meta, upd, upd_t, block_mask, cot, f_other = held
     sends = jnp.concatenate([p[ROWS : ROWS + 1, :nodes] for p in column])
     sends = sends.astype(jnp.int32).reshape(-1)
     outgoing = provide(dims, pos, sends, column)
-    outgoing, later = lax.optimization_barrier((outgoing, pos))
+    outgoing, later, query_rel = lax.optimization_barrier((outgoing, pos, query_rel))
+    query_vec = query_vectors(rel_table, query_rel)
+    first_table = relation_table(query_vec, rel_proj[0])
     b_own, b_send = split_weights(later, weights)
     row_ids = node * (NB_DEV * BLK) + (
         jnp.arange(NB_DEV, dtype=jnp.int32)[:, None] * BLK
@@ -533,8 +548,8 @@
             table = relation_table(vectors, rel_proj[l])
             rec_own, table = lax.optimization_barrier((rec_own, table))
         else:
-            rec_own, bound, b_own, b_send = lax.optimization_barrier(
-                (rec_own, bound, b_own, b_send)
+            rec_own, bound, b_own, b_send, table = lax.optimization_barrier(
+                (rec_own, bound, b_own, b_send, table)
             )
         tables.append(table)
         rec_own = rec_own.reshape(nodes, HB, COLS)
@@ -568,9 +583,8 @@
         parts = lax.all_to_all(combined, "z", 0, 0, tiled=True)
         if whole:
             relation = whole[0] + swap(whole[0])
-            last_proj = project(query_vec, relation, scale_factor)
             last_upd = update_sum(relation, scale_factor)
-            parts, last_proj, last_upd = lax.optimization_barrier((parts, last_proj, last_upd))
+            parts, last_relation, last_upd = lax.optimization_barrier((parts, relation, last_upd))
         more = (aux, upd_t[0], block_mask) if l else ()
         made = collect(chunk, parts, grad, more)
         grad, rel = made[:2]
@@ -579,7 +593,7 @@
         passed = (rel,) if l else ()
     relation = gather_relations(dims, rel + swap(rel))
 
-    proj = jnp.stack([project(query_vec, relation, scale_factor), last_proj])
+    proj = project(query_vec, [relation, last_relation], scale_factor)
     upds = jnp.stack([update_sum(relation, scale_factor), last_upd])
     final_state = whole_rows(core, state, swap(state))
     grad_state = whole_rows(core, grad, swap(grad))

time: 311 us -> 307 us (0.987)
  matrix products: 8.6 us -> 2.51 us
    dot_general x2 -> x0, matrix products: 3.95 us -> none  [project(): product = jnp.dot(query_vec.T, flat, precision=EXACT_MATMUL)]
    pallas_call x0 -> x1, Pallas kernels: none -> 3.24 us  [project(): pl.pallas_call(functools.partial(project_kernel, scale_factor), out_shape...]
  transfers between devices with their start and end apart: 30 -> 30, of which waited for: 19 -> 18; matrix products, arithmetic and copies ran while one was open for 4% -> 4% of each run, Pallas kernels for 6% -> 6%
where the time goes in v3:
time: 307 us; the launch traced here: 306 us
  waiting for transfers between devices  101 us (33%)
  starting transfers between devices  70 us (23%)
  blocking collectives  68.2 us (22%)
  Pallas kernels  50.9 us (17%)
  local copies, waits for them, and re-layouts  6.92 us (2%)
  other arithmetic  4.16 us (1%)
    all_to_all x2, blocking collectives, body(): arrived = lax.all_to_all(sent, ('x', 'y'), 0, 0, tiled=True)  68.2 us
    all_to_all x2, waiting for transfers between devices, body(): rec_own = lax.all_to_all(outgoing, ('x', 'y'), 0, 0, tiled=True)  33.4 us
    all_to_all x2, waiting for transfers between devices, body(): parts = lax.all_to_all(combined, 'z', 0, 0, tiled=True)  31.4 us
    ppermute x11, starting transfers between devices, swap(): return lax.ppermute(value, 'c', SWAP)  25.7 us
    ppermute x14, starting transfers between devices, shift(): lax.ppermute(value, axis, [(s, (s + k) % count) for s in range(count)])  17.8 us
    ppermute x14, waiting for transfers between devices, shift(): lax.ppermute(value, axis, [(s, (s + k) % count) for s in range(count)])  16.7 us
    pallas_call x2, Pallas kernels, forward(): pl.pallas_call(functools.partial(forward_kernel, last, tiles), out_shape=...  14.5 us
    pallas_call x2, Pallas kernels, backward(): pl.pallas_call(functools.partial(backward_kernel, dims, tiles, chunk), ou...  12.3 us
  transfers between devices with their start and end apart: 30, of which 18 were waited for; matrix products, arithmetic and copies ran while one was open for 4% of the time, Pallas kernels for 6%

profile of v3, /device:TPU:1, one launch (start us, length us, event | category | flops | bytes accessed | tf_op | source)
XLA Modules:
  0.0 305.8 jit_solution(14689326715678723882)
XLA Ops:
  4.7 3.9 %collective-permute-start.4 = (bf16[272,128]{1,0:T(8,128)(2,1)S(1)}, bf16[272,128]{1,0:T(8,128)(2,1)S(1)}, u32[]{:S(2)}, u32[]{:S(2)}) collective-permute-start(bf16[272,128]{1,0:T(8,128)(2,1)S(1)} %fusion.7.refs_0_), channel_id=1, source_target_pairs={{0,56},{8,0},{16,8},{24,16},{32,24},{40,32},{48,40},{56,48},{1,57}... | collective-permute-start | bytes 208904 | tf_op jit(solution)/shard_map/ppermute | solution.py:464
  22.9 4.3 %collective-permute-done.3.refs_4_ = bf16[272,128]{1,0:T(8,128)(2,1)S(1)} collective-permute-done((bf16[272,128]{1,0:T(8,128)(2,1)S(1)}, bf16[272,128]{1,0:T(8,128)(2,1)S(1)}, u32[]{:S(2)}, u32[]{:S(2)}) %collective-permute-start.3) | collective-permute-done | bytes 69664 | tf_op jit(solution)/shard_map/ppermute | solution.py:464
  29.4 6.9 %all-to-all-start = ((bf16[16,8,64,128]{3,2,1,0:T(8,128)(2,1)}), bf16[16,8,64,128]{3,2,1,0:T(8,128)(2,1)S(1)}, u32[]{:S(2)}, u32[]{:S(2)}) async-start(bf16[16,8,64,128]{3,2,1,0:T(8,128)(2,1)} %provide.2), calls=%async_computation | async-start | bytes 4194304 | tf_op jit(solution)/shard_map/all_to_all | solution.py:546
  37.0 9.7 %split_weights.1 = (bf16[192,64,128]{2,1,0:T(8,128)(2,1)S(1)}, bf16[192,64,128]{2,1,0:T(8,128)(2,1)}) custom-call(s32[4]{0:T(128)S(1)} %pad_add_fusion.1.pos, bf16[192,128,128]{2,1,0:T(8,128)(2,1)} %bitcast.84), custom_call_target="tpu_custom_call" | custom-call | bytes 12582912 | tf_op jit(solution)/shard_map/split_weights/pallas_call | solution.py:120
  49.5 11.9 %all-to-all-done = bf16[16,8,64,128]{3,2,1,0:T(8,128)(2,1)S(1)} async-done(((bf16[16,8,64,128]{3,2,1,0:T(8,128)(2,1)}), bf16[16,8,64,128]{3,2,1,0:T(8,128)(2,1)S(1)}, u32[]{:S(2)}, u32[]{:S(2)}) %all-to-all-start) | async-done | bytes 2097184 | tf_op jit(solution)/shard_map/all_to_all | solution.py:546
  61.4 6.0 %collective-permute-start.9 = (bf16[128,64,128]{2,1,0:T(8,128)(2,1)S(1)}, bf16[128,64,128]{2,1,0:T(8,128)(2,1)S(1)}, u32[]{:S(2)}, u32[]{:S(2)}) collective-permute-start(bf16[128,64,128]{2,1,0:T(8,128)(2,1)S(1)} %bitcast.71), channel_id=1, source_target_pairs={{0,1},{1,0},{2,3},{3,2},{4,5},{5,4},{6,7},{7,6},{8,9},{9,8},{10,11... | collective-permute-start | bytes 6291464 | tf_op jit(solution)/shard_map/ppermute | solution.py:490
  67.4 3.8 %collective-permute-done.9.rec_other = bf16[128,64,128]{2,1,0:T(8,128)(2,1)S(1)} collective-permute-done((bf16[128,64,128]{2,1,0:T(8,128)(2,1)S(1)}, bf16[128,64,128]{2,1,0:T(8,128)(2,1)S(1)}, u32[]{:S(2)}, u32[]{:S(2)}) %collective-permute-start.9) | collective-permute-done | bytes 2097184 | tf_op jit(solution)/shard_map/ppermute | solution.py:490
  71.6 6.6 %forward_first.1 = (bf16[256,128]{1,0:T(8,128)(2,1)S(1)}, f32[2,256,128]{2,1,0:T(8,128)}) custom-call(s32[1536]{0:T(1024)S(1)} %reshape.408.meta, s32[4]{0:T(128)S(1)} %pad_add_fusion.1.pos, bf16[128,64,128]{2,1,0:T(8,128)(2,1)S(1)} %bitcast.72, bf16[128,64,128]{2,1,0:T(8,128)(2,1)S(1)} %collective-permute-done.9.rec_other, bf16[192,128,128]{2,1,0:T(8,128)(2,1)} %bitcast.85, ...), custom_call_target="tpu_custom_call" | custom-call | tf_op jit(solution)/shard_map/forward_first/pallas_call | solution.py:276
  91.7 4.3 %collective-permute-done.13.refs_4_ = bf16[256,128]{1,0:T(8,128)(2,1)S(1)} collective-permute-done((bf16[256,128]{1,0:T(8,128)(2,1)S(1)}, bf16[256,128]{1,0:T(8,128)(2,1)S(1)}, u32[]{:S(2)}, u32[]{:S(2)}) %collective-permute-start.13) | collective-permute-done | bytes 65568 | tf_op jit(solution)/shard_map/ppermute | solution.py:464
  98.1 4.5 %all-to-all-start.1 = ((bf16[16,8,64,128]{3,2,1,0:T(8,128)(2,1)}), bf16[16,8,64,128]{3,2,1,0:T(8,128)(2,1)}, u32[]{:S(2)}, u32[]{:S(2)}) async-start(bf16[16,8,64,128]{3,2,1,0:T(8,128)(2,1)} %provide.3), calls=%async_computation.1 | async-start | bytes 4194304 | tf_op jit(solution)/shard_map/all_to_all | solution.py:546
  104.9 21.5 %all-to-all-done.1 = bf16[16,8,64,128]{3,2,1,0:T(8,128)(2,1)} async-done(((bf16[16,8,64,128]{3,2,1,0:T(8,128)(2,1)}), bf16[16,8,64,128]{3,2,1,0:T(8,128)(2,1)}, u32[]{:S(2)}, u32[]{:S(2)}) %all-to-all-start.1) | async-done | bytes 2097184 | tf_op jit(solution)/shard_map/all_to_all | solution.py:546
  126.4 6.7 %collective-permute-start.18 = (bf16[128,64,128]{2,1,0:T(8,128)(2,1)}, bf16[128,64,128]{2,1,0:T(8,128)(2,1)}, u32[]{:S(2)}, u32[]{:S(2)}) collective-permute-start(bf16[128,64,128]{2,1,0:T(8,128)(2,1)} %bitcast.25.rec_own), channel_id=1, source_target_pairs={{0,1},{1,0},{2,3},{3,2},{4,5},{5,4},{6,7},{7,6},{8,9},{9,8},{10,11... | collective-permute-start | bytes 6291464 | tf_op jit(solution)/shard_map/ppermute | solution.py:490
  133.2 4.0 %collective-permute-done.18.rec_other = bf16[128,64,128]{2,1,0:T(8,128)(2,1)} collective-permute-done((bf16[128,64,128]{2,1,0:T(8,128)(2,1)}, bf16[128,64,128]{2,1,0:T(8,128)(2,1)}, u32[]{:S(2)}, u32[]{:S(2)}) %collective-permute-start.18) | collective-permute-done | bytes 2097184 | tf_op jit(solution)/shard_map/ppermute | solution.py:490
  137.2 7.9 %forward_last.1 = (bf16[256,128]{1,0:T(8,128)(2,1)S(1)}, bf16[256,128]{1,0:T(8,128)(2,1)S(1)}, f32[32,128]{1,0:T(8,128)S(1)}) custom-call(s32[1536]{0:T(1024)S(1)} %reshape.408.meta, s32[4]{0:T(128)S(1)} %pad_add_fusion.1.pos, bf16[128,64,128]{2,1,0:T(8,128)(2,1)} %bitcast.25.rec_own, bf16[128,64,128]{2,1,0:T(8,128)(2,1)} %collective-permute-done.18.rec_other, ...), custom_call_target="tpu_custom_call" | custom-call | tf_op jit(solution)/shard_map/forward_last/pallas_call | solution.py:276
  146.5 6.9 %backward.2 = bf16[16,560,128]{2,1,0:T(8,128)(2,1)S(1)} custom-call(s32[1536]{0:T(1024)S(1)} %reshape.408.meta, s32[4]{0:T(128)S(1)} %pad_add_fusion.1.pos, bf16[128,64,128]{2,1,0:T(8,128)(2,1)} %bitcast.25.rec_own, bf16[192,64,128]{2,1,0:T(8,128)(2,1)} %copy-done.1, bf16[192,64,128]{2,1,0:T(8,128)(2,1)} %collective-permute-done.17.w_other, ...), custom_call_target="tpu_custom_call" | custom-call | tf_op jit(solution)/shard_map/backward/pallas_call | solution.py:342
  153.4 33.4 %all_to_all.35.arrived = bf16[16,560,128]{2,1,0:T(8,128)(2,1)S(1)} all-to-all(bf16[16,560,128]{2,1,0:T(8,128)(2,1)S(1)} %backward.2), channel_id=1, replica_groups=mesh['x'=4,'z'=8,'y'=4,'c'=2] {'x','y'}, dimensions={0} | all-to-all | bytes 4587520 | tf_op jit(solution)/shard_map/all_to_all | solution.py:581
  189.2 7.4 %all-to-all-start.3 = ((bf16[8,304,128]{2,1,0:T(8,128)(2,1)}), bf16[8,304,128]{2,1,0:T(8,128)(2,1)S(1)}, u32[]{:S(2)}, u32[]{:S(2)}) async-start(bf16[8,304,128]{2,1,0:T(8,128)(2,1)} %combine.2), calls=%async_computation.3 | async-start | bytes 1245184 | tf_op jit(solution)/shard_map/all_to_all | solution.py:583
  196.7 17.7 %all-to-all-done.3.parts = bf16[8,304,128]{2,1,0:T(8,128)(2,1)S(1)} async-done(((bf16[8,304,128]{2,1,0:T(8,128)(2,1)}), bf16[8,304,128]{2,1,0:T(8,128)(2,1)S(1)}, u32[]{:S(2)}, u32[]{:S(2)}) %all-to-all-start.3) | async-done | bytes 622624 | tf_op jit(solution)/shard_map/all_to_all | solution.py:583
  219.5 5.5 %backward.3 = bf16[16,608,128]{2,1,0:T(8,128)(2,1)S(1)} custom-call(s32[1536]{0:T(1024)S(1)} %reshape.408.meta, s32[4]{0:T(128)S(1)} %pad_add_fusion.1.pos, bf16[128,64,128]{2,1,0:T(8,128)(2,1)S(1)} %bitcast.73, bf16[192,64,128]{2,1,0:T(8,128)(2,1)} %copy-done.1, bf16[192,64,128]{2,1,0:T(8,128)(2,1)} %collective-permute-done.17.w_other, ...), custom_call_target="tpu_custom_call" | custom-call | tf_op jit(solution)/shard_map/backward/pallas_call | solution.py:342
  225.0 34.8 %all_to_all.36.arrived = bf16[16,608,128]{2,1,0:T(8,128)(2,1)S(1)} all-to-all(bf16[16,608,128]{2,1,0:T(8,128)(2,1)S(1)} %backward.3), channel_id=1, replica_groups=mesh['x'=4,'z'=8,'y'=4,'c'=2] {'x','y'}, dimensions={0} | all-to-all | bytes 4980736 | tf_op jit(solution)/shard_map/all_to_all | solution.py:581
  262.0 3.5 %all-to-all-start.5 = ((bf16[8,304,128]{2,1,0:T(8,128)(2,1)}), bf16[8,304,128]{2,1,0:T(8,128)(2,1)S(1)}, u32[]{:S(2)}, u32[]{:S(2)}) async-start(bf16[8,304,128]{2,1,0:T(8,128)(2,1)} %get-tuple-element.110), calls=%async_computation.5 | async-start | bytes 1245184 | tf_op jit(solution)/shard_map/all_to_all | solution.py:583
  269.5 13.7 %all-to-all-done.5.parts = bf16[8,304,128]{2,1,0:T(8,128)(2,1)S(1)} async-done(((bf16[8,304,128]{2,1,0:T(8,128)(2,1)}), bf16[8,304,128]{2,1,0:T(8,128)(2,1)S(1)}, u32[]{:S(2)}, u32[]{:S(2)}) %all-to-all-start.5) | async-done | bytes 622624 | tf_op jit(solution)/shard_map/all_to_all | solution.py:583
  288.2 4.2 %all-to-all-start.6 = ((f32[16,48,128]{2,1,0:T(8,128)}), f32[16,48,128]{2,1,0:T(8,128)S(1)}, u32[]{:S(2)}, u32[]{:S(2)}) async-start(f32[16,48,128]{2,1,0:T(8,128)} %broadcast_in_dim.2), calls=%async_computation.6 | async-start | bytes 786432 | tf_op jit(solution)/shard_map/all_to_all | solution.py:443
  293.9 7.9 %all-to-all-done.6 = f32[16,48,128]{2,1,0:T(8,128)S(1)} async-done(((f32[16,48,128]{2,1,0:T(8,128)}), f32[16,48,128]{2,1,0:T(8,128)S(1)}, u32[]{:S(2)}, u32[]{:S(2)}) %all-to-all-start.6) | async-done | bytes 393248 | tf_op jit(solution)/shard_map/all_to_all | solution.py:443
  (131 shorter events, 67.1 us)
Async XLA Ops:
  0.6 26.5 %collective-permute-start.8 = (bf16[192,128,128]{2,1,0:T(8,128)(2,1)}, bf16[192,128,128]{2,1,0:T(8,128)(2,1)}, u32[]{:S(2)}, u32[]{:S(2)}) collective-permute-start(bf16[192,128,128]{2,1,0:T(8,128)(2,1)} %bitcast.83), channel_id=1, source_target_pairs={{0,1},{1,0},{2,3},{3,2},{4,5},{5,4},{6,7},{7,6},{8,9},{9,8},{10,11... | collective-permute-start | bytes 18874376 | tf_op jit(solution)/shard_map/ppermute | solution.py:490
  4.7 8.8 %collective-permute-start = (bf16[272,128]{1,0:T(8,128)(2,1)S(1)}, bf16[272,128]{1,0:T(8,128)(2,1)S(1)}, u32[]{:S(2)}, u32[]{:S(2)}) collective-permute-start(bf16[272,128]{1,0:T(8,128)(2,1)S(1)} %fusion.7.refs_0_), channel_id=1, source_target_pairs={{0,8},{8,16},{16,24},{24,32},{32,40},{40,48},{48,56},{56,0},{1,9},... | collective-permute-start | bytes 208904 | tf_op jit(solution)/shard_map/ppermute | solution.py:464
  4.7 9.6 %collective-permute-start.4 = (bf16[272,128]{1,0:T(8,128)(2,1)S(1)}, bf16[272,128]{1,0:T(8,128)(2,1)S(1)}, u32[]{:S(2)}, u32[]{:S(2)}) collective-permute-start(bf16[272,128]{1,0:T(8,128)(2,1)S(1)} %fusion.7.refs_0_), channel_id=1, source_target_pairs={{0,56},{8,0},{16,8},{24,16},{32,24},{40,32},{48,40},{56,48},{1,57}... | collective-permute-start | bytes 208904 | tf_op jit(solution)/shard_map/ppermute | solution.py:464
  10.9 12.0 %collective-permute-start.7 = (s32[4,192]{1,0:T(4,128)S(1)}, s32[4,192]{1,0:T(4,128)S(1)}, u32[]{:S(2)}, u32[]{:S(2)}) collective-permute-start(s32[4,192]{1,0:T(4,128)S(1)} %add_add_fusion), channel_id=1, source_target_pairs={{0,1},{1,0},{2,3},{3,2},{4,5},{5,4},{6,7},{7,6},{8,9},{9,8},{10,11... | collective-permute-start | bytes 9224 | tf_op jit(solution)/shard_map/ppermute | solution.py:490
  13.4 5.0 %collective-permute-start.1 = (bf16[272,128]{1,0:T(8,128)(2,1)S(1)}, bf16[272,128]{1,0:T(8,128)(2,1)S(1)}, u32[]{:S(2)}, u32[]{:S(2)}) collective-permute-start(bf16[272,128]{1,0:T(8,128)(2,1)S(1)} %collective-permute-done.refs_1_), channel_id=1, source_target_pairs={{0,8},{8,16},{16,24},{24,32},{32,40},{40,48},{48,56},{56,0},{1,9},... | collective-permute-start | bytes 208904 | tf_op jit(solution)/shard_map/ppermute | solution.py:464
  18.4 4.4 %collective-permute-start.2 = (bf16[272,128]{1,0:T(8,128)(2,1)S(1)}, bf16[272,128]{1,0:T(8,128)(2,1)S(1)}, u32[]{:S(2)}, u32[]{:S(2)}) collective-permute-start(bf16[272,128]{1,0:T(8,128)(2,1)S(1)} %collective-permute-done.1.refs_2_), channel_id=1, source_target_pairs={{0,8},{8,16},{16,24},{24,32},{32,40},{40,48},{48,56},{56,0},{1,9},... | collective-permute-start | bytes 208904 | tf_op jit(solution)/shard_map/ppermute | solution.py:464
  18.5 4.4 %collective-permute-start.6 = (bf16[272,128]{1,0:T(8,128)(2,1)S(1)}, bf16[272,128]{1,0:T(8,128)(2,1)S(1)}, u32[]{:S(2)}, u32[]{:S(2)}) collective-permute-start(bf16[272,128]{1,0:T(8,128)(2,1)S(1)} %collective-permute-done.5.refs_6_), channel_id=1, source_target_pairs={{0,56},{8,0},{16,8},{24,16},{32,24},{40,32},{48,40},{56,48},{1,57}... | collective-permute-start | bytes 208904 | tf_op jit(solution)/shard_map/ppermute | solution.py:464
  22.8 4.4 %collective-permute-start.3 = (bf16[272,128]{1,0:T(8,128)(2,1)S(1)}, bf16[272,128]{1,0:T(8,128)(2,1)S(1)}, u32[]{:S(2)}, u32[]{:S(2)}) collective-permute-start(bf16[272,128]{1,0:T(8,128)(2,1)S(1)} %collective-permute-done.2.refs_3_), channel_id=1, source_target_pairs={{0,8},{8,16},{16,24},{24,32},{32,40},{40,48},{48,56},{56,0},{1,9},... | collective-permute-start | bytes 208904 | tf_op jit(solution)/shard_map/ppermute | solution.py:464
  29.4 32.0 %all-to-all-start = ((bf16[16,8,64,128]{3,2,1,0:T(8,128)(2,1)}), bf16[16,8,64,128]{3,2,1,0:T(8,128)(2,1)S(1)}, u32[]{:S(2)}, u32[]{:S(2)}) async-start(bf16[16,8,64,128]{3,2,1,0:T(8,128)(2,1)} %provide.2), calls=%async_computation | async-start | bytes 4194304 | tf_op jit(solution)/shard_map/all_to_all | solution.py:546
  61.4 9.8 %collective-permute-start.9 = (bf16[128,64,128]{2,1,0:T(8,128)(2,1)S(1)}, bf16[128,64,128]{2,1,0:T(8,128)(2,1)S(1)}, u32[]{:S(2)}, u32[]{:S(2)}) collective-permute-start(bf16[128,64,128]{2,1,0:T(8,128)(2,1)S(1)} %bitcast.71), channel_id=1, source_target_pairs={{0,1},{1,0},{2,3},{3,2},{4,5},{5,4},{6,7},{7,6},{8,9},{9,8},{10,11... | collective-permute-start | bytes 6291464 | tf_op jit(solution)/shard_map/ppermute | solution.py:490
  71.2 24.8 %collective-permute-start.17 = (bf16[192,64,128]{2,1,0:T(8,128)(2,1)}, bf16[192,64,128]{2,1,0:T(8,128)(2,1)}, u32[]{:S(2)}, u32[]{:S(2)}) collective-permute-start(bf16[192,64,128]{2,1,0:T(8,128)(2,1)} %get-tuple-element.83), channel_id=1, source_target_pairs={{0,1},{1,0},{2,3},{3,2},{4,5},{5,4},{6,7},{7,6},{8,9},{9,8},{10,11... | collective-permute-start | bytes 9437192 | tf_op jit(solution)/shard_map/ppermute | solution.py:490
  78.2 4.8 %collective-permute-start.10 = (bf16[256,128]{1,0:T(8,128)(2,1)S(1)}, bf16[256,128]{1,0:T(8,128)(2,1)S(1)}, u32[]{:S(2)}, u32[]{:S(2)}) collective-permute-start(bf16[256,128]{1,0:T(8,128)(2,1)S(1)} %get-tuple-element.84.refs_0_.state), channel_id=1, source_target_pairs={{0,8},{8,16},{16,24},{24,32},{32,40},{40,48},{48,56},{56,0},{1,9},... | collective-permute-start | bytes 196616 | tf_op jit(solution)/shard_map/ppermute | solution.py:464
  78.2 4.8 %collective-permute-start.14 = (bf16[256,128]{1,0:T(8,128)(2,1)S(1)}, bf16[256,128]{1,0:T(8,128)(2,1)S(1)}, u32[]{:S(2)}, u32[]{:S(2)}) collective-permute-start(bf16[256,128]{1,0:T(8,128)(2,1)S(1)} %get-tuple-element.84.refs_0_.state), channel_id=1, source_target_pairs={{0,56},{8,0},{16,8},{24,16},{32,24},{40,32},{48,40},{56,48},{1,57}... | collective-permute-start | bytes 196616 | tf_op jit(solution)/shard_map/ppermute | solution.py:464
  83.0 4.3 %collective-permute-start.11 = (bf16[256,128]{1,0:T(8,128)(2,1)S(1)}, bf16[256,128]{1,0:T(8,128)(2,1)S(1)}, u32[]{:S(2)}, u32[]{:S(2)}) collective-permute-start(bf16[256,128]{1,0:T(8,128)(2,1)S(1)} %collective-permute-done.10.refs_1_), channel_id=1, source_target_pairs={{0,8},{8,16},{16,24},{24,32},{32,40},{40,48},{48,56},{56,0},{1,9},... | collective-permute-start | bytes 196616 | tf_op jit(solution)/shard_map/ppermute | solution.py:464
  83.0 4.3 %collective-permute-start.15 = (bf16[256,128]{1,0:T(8,128)(2,1)S(1)}, bf16[256,128]{1,0:T(8,128)(2,1)S(1)}, u32[]{:S(2)}, u32[]{:S(2)}) collective-permute-start(bf16[256,128]{1,0:T(8,128)(2,1)S(1)} %collective-permute-done.14.refs_7_), channel_id=1, source_target_pairs={{0,56},{8,0},{16,8},{24,16},{32,24},{40,32},{48,40},{56,48},{1,57}... | collective-permute-start | bytes 196616 | tf_op jit(solution)/shard_map/ppermute | solution.py:464
  87.3 4.3 %collective-permute-start.12 = (bf16[256,128]{1,0:T(8,128)(2,1)S(1)}, bf16[256,128]{1,0:T(8,128)(2,1)S(1)}, u32[]{:S(2)}, u32[]{:S(2)}) collective-permute-start(bf16[256,128]{1,0:T(8,128)(2,1)S(1)} %collective-permute-done.11.refs_2_), channel_id=1, source_target_pairs={{0,8},{8,16},{16,24},{24,32},{32,40},{40,48},{48,56},{56,0},{1,9},... | collective-permute-start | bytes 196616 | tf_op jit(solution)/shard_map/ppermute | solution.py:464
  87.3 4.3 %collective-permute-start.16 = (bf16[256,128]{1,0:T(8,128)(2,1)S(1)}, bf16[256,128]{1,0:T(8,128)(2,1)S(1)}, u32[]{:S(2)}, u32[]{:S(2)}) collective-permute-start(bf16[256,128]{1,0:T(8,128)(2,1)S(1)} %collective-permute-done.15.refs_6_), channel_id=1, source_target_pairs={{0,56},{8,0},{16,8},{24,16},{32,24},{40,32},{48,40},{56,48},{1,57}... | collective-permute-start | bytes 196616 | tf_op jit(solution)/shard_map/ppermute | solution.py:464
  98.1 28.3 %all-to-all-start.1 = ((bf16[16,8,64,128]{3,2,1,0:T(8,128)(2,1)}), bf16[16,8,64,128]{3,2,1,0:T(8,128)(2,1)}, u32[]{:S(2)}, u32[]{:S(2)}) async-start(bf16[16,8,64,128]{3,2,1,0:T(8,128)(2,1)} %provide.3), calls=%async_computation.1 | async-start | bytes 4194304 | tf_op jit(solution)/shard_map/all_to_all | solution.py:546
  126.4 10.8 %collective-permute-start.18 = (bf16[128,64,128]{2,1,0:T(8,128)(2,1)}, bf16[128,64,128]{2,1,0:T(8,128)(2,1)}, u32[]{:S(2)}, u32[]{:S(2)}) collective-permute-start(bf16[128,64,128]{2,1,0:T(8,128)(2,1)} %bitcast.25.rec_own), channel_id=1, source_target_pairs={{0,1},{1,0},{2,3},{3,2},{4,5},{5,4},{6,7},{7,6},{8,9},{9,8},{10,11... | collective-permute-start | bytes 6291464 | tf_op jit(solution)/shard_map/ppermute | solution.py:490
  189.2 25.2 %all-to-all-start.3 = ((bf16[8,304,128]{2,1,0:T(8,128)(2,1)}), bf16[8,304,128]{2,1,0:T(8,128)(2,1)S(1)}, u32[]{:S(2)}, u32[]{:S(2)}) async-start(bf16[8,304,128]{2,1,0:T(8,128)(2,1)} %combine.2), calls=%async_computation.3 | async-start | bytes 1245184 | tf_op jit(solution)/shard_map/all_to_all | solution.py:583
  262.0 21.2 %all-to-all-start.5 = ((bf16[8,304,128]{2,1,0:T(8,128)(2,1)}), bf16[8,304,128]{2,1,0:T(8,128)(2,1)S(1)}, u32[]{:S(2)}, u32[]{:S(2)}) async-start(bf16[8,304,128]{2,1,0:T(8,128)(2,1)} %get-tuple-element.110), calls=%async_computation.5 | async-start | bytes 1245184 | tf_op jit(solution)/shard_map/all_to_all | solution.py:583
  268.0 18.3 %collective-permute-start.19 = (bf16[256,128]{1,0:T(8,128)(2,1)S(1)}, bf16[256,128]{1,0:T(8,128)(2,1)S(1)}, u32[]{:S(2)}, u32[]{:S(2)}) collective-permute-start(bf16[256,128]{1,0:T(8,128)(2,1)S(1)} %copy-done.3), channel_id=1, source_target_pairs={{0,1},{1,0},{2,3},{3,2},{4,5},{5,4},{6,7},{7,6},{8,9},{9,8},{10,11... | collective-permute-start | bytes 196616 | tf_op jit(solution)/shard_map/ppermute | solution.py:490
  283.3 9.8 %collective-permute-start.23 = (f32[256,128]{1,0:T(8,128)S(1)}, f32[256,128]{1,0:T(8,128)S(1)}, u32[]{:S(2)}, u32[]{:S(2)}) collective-permute-start(f32[256,128]{1,0:T(8,128)S(1)} %get-tuple-element.114), channel_id=1, source_target_pairs={{0,1},{1,0},{2,3},{3,2},{4,5},{5,4},{6,7},{7,6},{8,9},{9,8},{10,11... | collective-permute-start | bytes 393224 | tf_op jit(solution)/shard_map/ppermute | solution.py:490
  288.2 13.5 %all-to-all-start.6 = ((f32[16,48,128]{2,1,0:T(8,128)}), f32[16,48,128]{2,1,0:T(8,128)S(1)}, u32[]{:S(2)}, u32[]{:S(2)}) async-start(f32[16,48,128]{2,1,0:T(8,128)} %broadcast_in_dim.2), calls=%async_computation.6 | async-start | bytes 786432 | tf_op jit(solution)/shard_map/all_to_all | solution.py:443
  (14 other events, 73.9 us)
